TPU v7x, 256 devices: a whole 4x4x8 slice. The times are simulated.
256 devices in a mesh: fsdp: 4 (over x), seq: 64 (over z, y, core).
Axes of the slice: x: 4, y: 4, z: 8, core: 2. Of those that a mesh axis runs over, the one named last changes fastest.
Arguments:
- tokens: bfloat16 [4, 16384, 4096], P('fsdp', 'seq'), may hold values from -6 to 6
- queries: bfloat16 [4, 16384, 4096], P('fsdp', 'seq'), may hold values from -70 to 70
- key_weight: bfloat16 [4096, 1024], P(('fsdp', 'seq')), may hold values from -0.09375 to 0.09375
- value_weight: bfloat16 [4096, 1024], P(('fsdp', 'seq')), may hold values from -0.09375 to 0.09375
- sorted_blocks: int32 [4, 8, 128], P('fsdp', None, 'seq'), may hold values from 0 to 127, as said below
Outputs:
- attended: bfloat16 [4, 16384, 4096], P('fsdp', 'seq')
Inputs may be any that keep to these rules, and one draw needn't show every extreme that they name: `sorted_blocks`: for each sequence and key-value head, a permutation of the 128 blocks. The 2 blocks of one device, over all key-value heads, name blocks that lie on one device at most 1 times, and for one head at most 1 times; both bounds are reached in every draw. Device d holds blocks d * 2 to d * 2 + 1.
All inputs are finite; a program needn't handle non-finite values.
Results may differ from a plain program's by a relative error of at most 0.012.
The roundings to bfloat16 on the way count: a program that leaves them out, or rounds other values in their place, can miss the bound.
Values may be sent and summed in bfloat16 or wider, within the bound.
A program may use at most 128 MiB of HBM per device.

v0:
```python
import math

import jax
import jax.numpy as jnp
from jax import lax
from jax.sharding import PartitionSpec as P

DH = 128
KVH = 8
GROUP = 4
BLOCK = 128


def shifted(value, axis, steps):
    count = lax.axis_size(axis)
    first, last = (max(0, -steps), min(count, count - steps))
    return lax.ppermute(value, axis, [(source, source + steps) for source in range(first, last)])


def fetch_blocks(kv_table, target_dev, target_row, devices, capacity, send_requests, send_blocks):
    item_count = target_dev.shape[0]
    item_order = jnp.arange(item_count, dtype=jnp.int32)
    same_dev = target_dev[:, None] == target_dev[None, :]
    earlier = item_order[None, :] < item_order[:, None]
    ranking = jnp.sum((same_dev & earlier).astype(jnp.int32), axis=1)
    dev_hit = target_dev[:, None, None] == jnp.arange(devices, dtype=jnp.int32)[None, :, None]
    slot_hit = ranking[:, None, None] == jnp.arange(capacity, dtype=jnp.int32)[None, None, :]
    requests = jnp.sum(jnp.where(dev_hit & slot_hit, (target_row + 1)[:, None, None], 0), axis=0)
    wanted = send_requests(requests)
    replies = jnp.take(kv_table, jnp.maximum(wanted - 1, 0), axis=0)
    replies = jnp.where((wanted > 0)[:, :, None, None], replies, jnp.zeros_like(replies))
    arrived = send_blocks(replies)
    arrived = arrived.reshape(devices * capacity, arrived.shape[2], arrived.shape[3])
    return jnp.take(arrived, target_dev * capacity + ranking, axis=0)


def local(tokens, queries, key_weight, value_weight, sorted_blocks):
    token_rows = tokens[0]
    local_tokens = token_rows.shape[0]
    local_blocks = local_tokens // BLOCK
    devices = lax.axis_size("seq")
    key_sums = jnp.dot(
        token_rows,
        lax.all_gather(key_weight, ("fsdp", "seq"), axis=0, tiled=True),
        preferred_element_type=jnp.float32,
    )
    value_sums = jnp.dot(
        token_rows,
        lax.all_gather(value_weight, ("fsdp", "seq"), axis=0, tiled=True),
        preferred_element_type=jnp.float32,
    )
    key_blocks = key_sums.astype(jnp.bfloat16).reshape(local_blocks, BLOCK, KVH, DH)
    value_blocks = value_sums.astype(jnp.bfloat16).reshape(local_blocks, BLOCK, KVH, DH)
    packed = jnp.concatenate([key_blocks, value_blocks], axis=3).transpose(2, 0, 1, 3)
    prev_edge = shifted(packed[:, local_blocks - 1], "seq", 1)
    preceding = jnp.concatenate([prev_edge[:, None], packed[:, : local_blocks - 1]], axis=1)
    targets = sorted_blocks[0]
    target_dev = targets // local_blocks
    target_slot = targets % local_blocks
    capacity = (local_blocks + devices - 1) // devices
    gathered_heads = []
    for kv_head in range(KVH):
        gathered_heads.append(
            fetch_blocks(
                packed[kv_head],
                target_dev[kv_head],
                target_slot[kv_head],
                devices,
                capacity,
                lambda payload: lax.all_to_all(
                    payload, "seq", split_axis=0, concat_axis=0, tiled=True
                ),
                lambda payload: lax.all_to_all(
                    payload, "seq", split_axis=0, concat_axis=0, tiled=True
                ),
            )
        )
    sorted_kv = jnp.stack(gathered_heads, axis=0)
    candidates = jnp.concatenate([packed, preceding, sorted_kv], axis=2)
    key_part = candidates[:, :, :, :DH]
    value_part = candidates[:, :, :, DH:]
    query_blocks = queries[0].reshape(local_blocks, BLOCK, KVH, GROUP, DH)
    scores = jnp.einsum(
        "bthge,hbke->hgbtk", query_blocks, key_part, preferred_element_type=jnp.float32
    ) * (1.0 / math.sqrt(DH))
    block_index = lax.axis_index("seq") * local_blocks + jnp.arange(local_blocks, dtype=jnp.int32)
    key_index = jnp.arange(3 * BLOCK, dtype=jnp.int32)
    blocked = (
        (block_index[:, None] == 0)
        & (key_index[None, :] >= BLOCK)
        & (key_index[None, :] < 2 * BLOCK)
    )
    scores = jnp.where(blocked[None, None, :, None, :], -1e30, scores)
    highest = jnp.max(scores, axis=-1, keepdims=True)
    raised = jnp.exp(scores - highest)
    weights = (raised / jnp.sum(raised, axis=-1, keepdims=True)).astype(jnp.bfloat16)
    result = jnp.einsum(
        "hgbtk,hbke->bthge", weights, value_part, preferred_element_type=jnp.float32
    )
    return result.astype(jnp.bfloat16).reshape(1, local_tokens, KVH * GROUP * DH)


def solution(mesh):
    placed = (
        P("fsdp", "seq", None),
        P("fsdp", "seq", None),
        P(("fsdp", "seq"), None),
        P(("fsdp", "seq"), None),
        P("fsdp", None, "seq"),
    )
    return jax.shard_map(
        local, mesh=mesh, in_specs=placed, out_specs=P("fsdp", "seq", None), check_vma=False
    )
```

profile of v0, /device:TPU:1, one launch (start us, length us, event | category | flops | bytes accessed | tf_op | source)
XLA Modules:
  0.0 1156.5 jit_solution(5378206535577151252)
XLA Ops:
  10.1 13.2 %all-to-all-start.14 = ((s32[64,1,1]{2,1,0:T(1,128)}), s32[64,1,1]{2,1,0:T(1,128)S(1)}, u32[]{:S(2)}, u32[]{:S(2)}) async-start(s32[64,1,1]{2,1,0:T(1,128)} %copy.82), calls=%async_computation.14 | async-start | bytes 65536 | tf_op jit(solution)/shard_map/all_to_all | solution.py:70
  33.3 10.3 all-to-all-start
  57.6 9.5 all-to-all-done.2
  71.7 62.1 %all-gather.3.cloned.1.call-done = bf16[4096,1024]{1,0:T(8,128)(2,1)} async-done(((bf16[16,1024]{1,0:T(8,128)(2,1)}), bf16[4096,1024]{1,0:T(8,128)(2,1)}) %all-gather.3.cloned.1.call-update) | async-done | bytes 8388624 | tf_op jit(solution)/shard_map/all_gather | solution.py:44
  139.5 6.9 all-to-all-start.6
  146.4 106.1 %all-gather.5.cloned.1.call-done = bf16[4096,1024]{1,0:T(8,128)(2,1)} async-done(((bf16[16,1024]{1,0:T(8,128)(2,1)}), bf16[4096,1024]{1,0:T(8,128)(2,1)}) %all-gather.5.cloned.1.call-update) | async-done | bytes 8388624 | tf_op jit(solution)/shard_map/all_gather | solution.py:49
  265.7 9.2 all-to-all-done.8
  318.3 85.4 %all-to-all-done.15 = bf16[64,1,128,256]{3,2,1,0:T(8,128)(2,1)} async-done(((bf16[64,1,128,256]{3,2,1,0:T(8,128)(2,1)}), bf16[64,1,128,256]{3,2,1,0:T(8,128)(2,1)}, u32[]{:S(2)}, u32[]{:S(2)}) %all-to-all-start.15) | async-done | bytes 4194336 | tf_op jit(solution)/shard_map/all_to_all | solution.py:73
  403.7 7.2 all-to-all-start.11
  420.1 85.4 %all-to-all-done.11 = bf16[64,1,128,256]{3,2,1,0:T(8,128)(2,1)} async-done(((bf16[64,1,128,256]{3,2,1,0:T(8,128)(2,1)}), bf16[64,1,128,256]{3,2,1,0:T(8,128)(2,1)}, u32[]{:S(2)}, u32[]{:S(2)}) %all-to-all-start.11) | async-done | bytes 4194336 | tf_op jit(solution)/shard_map/all_to_all | solution.py:73
  505.6 7.6 all-to-all-start.9
  522.4 85.2 %all-to-all-done.9 = bf16[64,1,128,256]{3,2,1,0:T(8,128)(2,1)} async-done(((bf16[64,1,128,256]{3,2,1,0:T(8,128)(2,1)}), bf16[64,1,128,256]{3,2,1,0:T(8,128)(2,1)}, u32[]{:S(2)}, u32[]{:S(2)}) %all-to-all-start.9) | async-done | bytes 4194336 | tf_op jit(solution)/shard_map/all_to_all | solution.py:73
  607.6 7.2 all-to-all-start.7
  624.0 85.5 %all-to-all-done.7 = bf16[64,1,128,256]{3,2,1,0:T(8,128)(2,1)} async-done(((bf16[64,1,128,256]{3,2,1,0:T(8,128)(2,1)}), bf16[64,1,128,256]{3,2,1,0:T(8,128)(2,1)}, u32[]{:S(2)}, u32[]{:S(2)}) %all-to-all-start.7) | async-done | bytes 4194336 | tf_op jit(solution)/shard_map/all_to_all | solution.py:73
  709.5 7.2 all-to-all-start.5
  726.0 85.5 %all-to-all-done.5 = bf16[64,1,128,256]{3,2,1,0:T(8,128)(2,1)} async-done(((bf16[64,1,128,256]{3,2,1,0:T(8,128)(2,1)}), bf16[64,1,128,256]{3,2,1,0:T(8,128)(2,1)}, u32[]{:S(2)}, u32[]{:S(2)}) %all-to-all-start.5) | async-done | bytes 4194336 | tf_op jit(solution)/shard_map/all_to_all | solution.py:73
  811.5 7.6 all-to-all-start.3
  828.3 85.3 %all-to-all-done.3 = bf16[64,1,128,256]{3,2,1,0:T(8,128)(2,1)} async-done(((bf16[64,1,128,256]{3,2,1,0:T(8,128)(2,1)}), bf16[64,1,128,256]{3,2,1,0:T(8,128)(2,1)}, u32[]{:S(2)}, u32[]{:S(2)}) %all-to-all-start.3) | async-done | bytes 4194336 | tf_op jit(solution)/shard_map/all_to_all | solution.py:73
  913.6 7.2 all-to-all-start.1
  930.2 85.3 %all-to-all-done.1 = bf16[64,1,128,256]{3,2,1,0:T(8,128)(2,1)} async-done(((bf16[64,1,128,256]{3,2,1,0:T(8,128)(2,1)}), bf16[64,1,128,256]{3,2,1,0:T(8,128)(2,1)}, u32[]{:S(2)}, u32[]{:S(2)}) %all-to-all-start.1) | async-done | bytes 4194336 | tf_op jit(solution)/shard_map/all_to_all | solution.py:73
  1015.5 7.2 all-to-all-start.13
  1058.8 59.7 %all-to-all-done.13 = bf16[64,1,128,256]{3,2,1,0:T(8,128)(2,1)} async-done(((bf16[64,1,128,256]{3,2,1,0:T(8,128)(2,1)}), bf16[64,1,128,256]{3,2,1,0:T(8,128)(2,1)}, u32[]{:S(2)}, u32[]{:S(2)}) %all-to-all-start.13) | async-done | bytes 4194336 | tf_op jit(solution)/shard_map/all_to_all | solution.py:73
  1123.3 9.2 fusion.80
  1132.5 7.9 convert_bitcast_fusion
  (152 shorter events, 199.3 us)
Async XLA Ops:
  6.5 127.2 %copy-start = (bf16[1,256,4096]{2,1,0:T(8,128)(2,1)S(1)}, bf16[1,256,4096]{2,1,0:T(8,128)(2,1)}, u32[]{:S(2)}) copy-start(bf16[1,256,4096]{2,1,0:T(8,128)(2,1)} %param.9) | copy-start | bytes 6291460
  6.5 127.2 %all-gather.3.cloned.1.call-start = ((), (), s32[]{:S(2)}) async-start(), calls=%async_computation.16 | async-start | bytes 8421376 | tf_op jit(solution)/shard_map/all_gather | solution.py:44
  7.3 245.3 %all-gather.5.cloned.1.call-start = ((), (), s32[]{:S(2)}) async-start(), calls=%async_computation.17 | async-start | bytes 8421376 | tf_op jit(solution)/shard_map/all_gather | solution.py:49
  10.1 23.2 %all-to-all-start.14 = ((s32[64,1,1]{2,1,0:T(1,128)}), s32[64,1,1]{2,1,0:T(1,128)S(1)}, u32[]{:S(2)}, u32[]{:S(2)}) async-start(s32[64,1,1]{2,1,0:T(1,128)} %copy.82), calls=%async_computation.14 | async-start | bytes 65536 | tf_op jit(solution)/shard_map/all_to_all | solution.py:70
  33.3 19.6 %all-to-all-start = ((s32[64,1,1]{2,1,0:T(1,128)}), s32[64,1,1]{2,1,0:T(1,128)S(1)}, u32[]{:S(2)}, u32[]{:S(2)}) async-start(s32[64,1,1]{2,1,0:T(1,128)} %copy.68), calls=%async_computation | async-start | bytes 65536 | tf_op jit(solution)/shard_map/all_to_all | solution.py:70
  52.9 14.1 %all-to-all-start.2 = ((s32[64,1,1]{2,1,0:T(1,128)}), s32[64,1,1]{2,1,0:T(1,128)S(1)}, u32[]{:S(2)}, u32[]{:S(2)}) async-start(s32[64,1,1]{2,1,0:T(1,128)} %copy.70), calls=%async_computation.2 | async-start | bytes 65536 | tf_op jit(solution)/shard_map/all_to_all | solution.py:70
  67.1 72.4 %all-to-all-start.4 = ((s32[64,1,1]{2,1,0:T(1,128)}), s32[64,1,1]{2,1,0:T(1,128)S(1)}, u32[]{:S(2)}, u32[]{:S(2)}) async-start(s32[64,1,1]{2,1,0:T(1,128)} %copy.72), calls=%async_computation.4 | async-start | bytes 65536 | tf_op jit(solution)/shard_map/all_to_all | solution.py:70
  139.5 119.2 %all-to-all-start.6 = ((s32[64,1,1]{2,1,0:T(1,128)}), s32[64,1,1]{2,1,0:T(1,128)S(1)}, u32[]{:S(2)}, u32[]{:S(2)}) async-start(s32[64,1,1]{2,1,0:T(1,128)} %copy.74), calls=%async_computation.6 | async-start | bytes 65536 | tf_op jit(solution)/shard_map/all_to_all | solution.py:70
  258.7 16.3 %all-to-all-start.8 = ((s32[64,1,1]{2,1,0:T(1,128)}), s32[64,1,1]{2,1,0:T(1,128)S(1)}, u32[]{:S(2)}, u32[]{:S(2)}) async-start(s32[64,1,1]{2,1,0:T(1,128)} %copy.76), calls=%async_computation.8 | async-start | bytes 65536 | tf_op jit(solution)/shard_map/all_to_all | solution.py:70
  275.0 14.2 %all-to-all-start.10 = ((s32[64,1,1]{2,1,0:T(1,128)}), s32[64,1,1]{2,1,0:T(1,128)S(1)}, u32[]{:S(2)}, u32[]{:S(2)}) async-start(s32[64,1,1]{2,1,0:T(1,128)} %copy.78), calls=%async_computation.10 | async-start | bytes 65536 | tf_op jit(solution)/shard_map/all_to_all | solution.py:70
  289.2 14.1 %all-to-all-start.12 = ((s32[64,1,1]{2,1,0:T(1,128)}), s32[64,1,1]{2,1,0:T(1,128)S(1)}, u32[]{:S(2)}, u32[]{:S(2)}) async-start(s32[64,1,1]{2,1,0:T(1,128)} %copy.80), calls=%async_computation.12 | async-start | bytes 65536 | tf_op jit(solution)/shard_map/all_to_all | solution.py:70
  303.3 100.3 %all-to-all-start.15 = ((bf16[64,1,128,256]{3,2,1,0:T(8,128)(2,1)}), bf16[64,1,128,256]{3,2,1,0:T(8,128)(2,1)}, u32[]{:S(2)}, u32[]{:S(2)}) async-start(bf16[64,1,128,256]{3,2,1,0:T(8,128)(2,1)} %fusion.13), calls=%async_computation.15 | async-start | bytes 8388608 | tf_op jit(solution)/shard_map/all_to_all | solution.py:73
  403.7 101.9 %all-to-all-start.11 = ((bf16[64,1,128,256]{3,2,1,0:T(8,128)(2,1)}), bf16[64,1,128,256]{3,2,1,0:T(8,128)(2,1)}, u32[]{:S(2)}, u32[]{:S(2)}) async-start(bf16[64,1,128,256]{3,2,1,0:T(8,128)(2,1)} %fusion.17), calls=%async_computation.11 | async-start | bytes 8388608 | tf_op jit(solution)/shard_map/all_to_all | solution.py:73
  505.6 102.1 %all-to-all-start.9 = ((bf16[64,1,128,256]{3,2,1,0:T(8,128)(2,1)}), bf16[64,1,128,256]{3,2,1,0:T(8,128)(2,1)}, u32[]{:S(2)}, u32[]{:S(2)}) async-start(bf16[64,1,128,256]{3,2,1,0:T(8,128)(2,1)} %fusion.19), calls=%async_computation.9 | async-start | bytes 8388608 | tf_op jit(solution)/shard_map/all_to_all | solution.py:73
  607.6 101.9 %all-to-all-start.7 = ((bf16[64,1,128,256]{3,2,1,0:T(8,128)(2,1)}), bf16[64,1,128,256]{3,2,1,0:T(8,128)(2,1)}, u32[]{:S(2)}, u32[]{:S(2)}) async-start(bf16[64,1,128,256]{3,2,1,0:T(8,128)(2,1)} %fusion.21), calls=%async_computation.7 | async-start | bytes 8388608 | tf_op jit(solution)/shard_map/all_to_all | solution.py:73
  709.5 101.9 %all-to-all-start.5 = ((bf16[64,1,128,256]{3,2,1,0:T(8,128)(2,1)}), bf16[64,1,128,256]{3,2,1,0:T(8,128)(2,1)}, u32[]{:S(2)}, u32[]{:S(2)}) async-start(bf16[64,1,128,256]{3,2,1,0:T(8,128)(2,1)} %fusion.23), calls=%async_computation.5 | async-start | bytes 8388608 | tf_op jit(solution)/shard_map/all_to_all | solution.py:73
  811.5 102.1 %all-to-all-start.3 = ((bf16[64,1,128,256]{3,2,1,0:T(8,128)(2,1)}), bf16[64,1,128,256]{3,2,1,0:T(8,128)(2,1)}, u32[]{:S(2)}, u32[]{:S(2)}) async-start(bf16[64,1,128,256]{3,2,1,0:T(8,128)(2,1)} %fusion.25), calls=%async_computation.3 | async-start | bytes 8388608 | tf_op jit(solution)/shard_map/all_to_all | solution.py:73
  913.6 101.9 %all-to-all-start.1 = ((bf16[64,1,128,256]{3,2,1,0:T(8,128)(2,1)}), bf16[64,1,128,256]{3,2,1,0:T(8,128)(2,1)}, u32[]{:S(2)}, u32[]{:S(2)}) async-start(bf16[64,1,128,256]{3,2,1,0:T(8,128)(2,1)} %fusion.27), calls=%async_computation.1 | async-start | bytes 8388608 | tf_op jit(solution)/shard_map/all_to_all | solution.py:73
  1015.5 103.1 %all-to-all-start.13 = ((bf16[64,1,128,256]{3,2,1,0:T(8,128)(2,1)}), bf16[64,1,128,256]{3,2,1,0:T(8,128)(2,1)}, u32[]{:S(2)}, u32[]{:S(2)}) async-start(bf16[64,1,128,256]{3,2,1,0:T(8,128)(2,1)} %fusion.15), calls=%async_computation.13 | async-start | bytes 8388608 | tf_op jit(solution)/shard_map/all_to_all | solution.py:73
  1028.8 92.6 %collective-permute-start = (bf16[8,128,256]{2,1,0:T(8,128)(2,1)}, bf16[8,128,256]{2,1,0:T(8,128)(2,1)S(1)}, u32[]{:S(2)}, u32[]{:S(2)}) collective-permute-start(bf16[8,128,256]{2,1,0:T(8,128)(2,1)} %get-tuple-element.39), channel_id=1, source_target_pairs={{0,1},{1,2},{2,3},{3,4},{4,5},{5,6},{6,7},{7,8},{8,9},{9,10},{10,1... | collective-permute-start | bytes 1572872 | tf_op jit(solution)/shard_map/ppermute | solution.py:17
  1132.5 16.9 %copy-start.1 = (bf16[1,256,4096]{2,1,0:T(8,128)(2,1)S(1)}, bf16[1,256,4096]{2,1,0:T(8,128)(2,1)}, u32[]{:S(2)}) copy-start(bf16[1,256,4096]{2,1,0:T(8,128)(2,1)} %param.9) | copy-start | bytes 6291460
Sparse Core Ops, SparseCore 0:
  11.1 122.6 all-gather.2
  137.5 115.0 all-gather.4
where the time goes:
time: 1170 us; the launch traced here: 1160 us
  waiting for transfers between devices  864 us (74%)
  starting transfers between devices  117 us (10%)
  local copies, waits for them, and re-layouts  66.5 us (6%)
  other arithmetic  66 us (6%)
  matrix products  28.5 us (2%)
  between operations  14.2 us (1%)
    all_to_all x16, waiting for transfers between devices, local(): lax.all_to_all(payload, 'seq', split_axis=0, concat_axis=0, tiled=True)  695 us
    all_to_all x16, starting transfers between devices, local(): lax.all_to_all(payload, 'seq', split_axis=0, concat_axis=0, tiled=True)  113 us
    all_gather x1, waiting for transfers between devices, local(): lax.all_gather(value_weight, ('fsdp', 'seq'), axis=0, tiled=True)  106 us
    all_gather x1, waiting for transfers between devices, local(): lax.all_gather(key_weight, ('fsdp', 'seq'), axis=0, tiled=True)  62.1 us
    select_n x8, other arithmetic, fetch_blocks(): jnp.where((wanted > 0)[:, :, None, None], replies, jnp.zeros_like(replies))  31.8 us
    gather x8, local copies, waits for them, and re-layouts, fetch_blocks(): return jnp.take(arrived, target_dev * capacity + ranking, axis=0)  23.9 us
  transfers between devices with their start and end apart: 19, of which 15 were waited for; matrix products, arithmetic and copies ran while one was open for 12% of the time, Pallas kernels for 0%

commit v1 on v0

v1 whole, which is shorter than its diff:
```python
import functools
import math

import jax
import jax.numpy as jnp
from jax import lax
from jax.experimental import pallas as pl
from jax.experimental.pallas import tpu as pltpu
from jax.sharding import PartitionSpec as P

DH = 128
KVH = 8
GROUP = 4
BLOCK = 128


def attend_kernel(table_ref, q_ref, own_ref, first_ref, edge_ref, sorted_ref, out_ref):
    block = pl.program_id(0)
    before = jnp.where(block == 0, edge_ref[0], first_ref[0, 0])
    candidates = jnp.concatenate([own_ref[0, 0], before, sorted_ref[0]], axis=0)
    queries = jnp.concatenate([q_ref[:, g * DH : (g + 1) * DH] for g in range(GROUP)], axis=0)
    scores = lax.dot_general(
        queries, candidates[:, :DH], (((1,), (1,)), ((), ())), preferred_element_type=jnp.float32
    ) * (math.log2(math.e) / math.sqrt(DH))
    index = lax.broadcasted_iota(jnp.int32, scores.shape, 1)
    start = (table_ref[2 * KVH] == 0) & (block == 0)
    blocked = start & (index >= BLOCK) & (index < 2 * BLOCK)
    scores = jnp.where(blocked, -1e30, scores)
    raised = jnp.exp2(scores - jnp.max(scores, axis=-1, keepdims=True))
    weights = (raised * (1.0 / jnp.sum(raised, axis=-1, keepdims=True))).astype(jnp.bfloat16)
    result = jnp.dot(weights, candidates[:, DH:], preferred_element_type=jnp.float32).astype(jnp.bfloat16)
    for g in range(GROUP):
        out_ref[:, g * DH : (g + 1) * DH] = result[g * BLOCK : (g + 1) * BLOCK]


def attend(table, queries, packed, edge, arrived):
    rows, width = queries.shape
    span = GROUP * DH
    kv = (1, 1, BLOCK, 2 * DH)
    return pl.pallas_call(
        attend_kernel,
        out_shape=jax.ShapeDtypeStruct((rows, width), jnp.bfloat16),
        grid_spec=pltpu.PrefetchScalarGridSpec(
            num_scalar_prefetch=1,
            grid=(rows // BLOCK, KVH),
            in_specs=[
                pl.BlockSpec((BLOCK, span), lambda b, h, t: (b, h)),
                pl.BlockSpec(kv, lambda b, h, t: (b, h, 0, 0)),
                pl.BlockSpec(kv, lambda b, h, t: (0, h, 0, 0)),
                pl.BlockSpec(kv[1:], lambda b, h, t: (h, 0, 0)),
                pl.BlockSpec(kv[1:], lambda b, h, t: (t[h * 2 + b], 0, 0)),
            ],
            out_specs=pl.BlockSpec((BLOCK, span), lambda b, h, t: (b, h)),
        ),
        name="attend",
    )(table, queries, packed, packed, edge, arrived)


def local(tokens, queries, key_weight, value_weight, sorted_blocks):
    token_rows = tokens[0]
    local_blocks = token_rows.shape[0] // BLOCK
    devices = lax.axis_size("seq")
    axes = ("fsdp", "seq")
    targets = sorted_blocks[0]
    target_dev = (targets // local_blocks).reshape(-1)
    item = (targets % local_blocks) * KVH + jnp.arange(KVH, dtype=jnp.int32)[:, None]
    hit = target_dev[:, None] == jnp.arange(devices, dtype=jnp.int32)[None, :]
    requests = jnp.sum(jnp.where(hit, (item.reshape(-1) + 1)[:, None], 0), axis=0)
    wanted = lax.all_to_all(requests[:, None], "seq", split_axis=0, concat_axis=0, tiled=True)[:, 0]
    keys = jnp.dot(
        token_rows, lax.all_gather(key_weight, axes, axis=0, tiled=True), preferred_element_type=jnp.float32
    )
    values = jnp.dot(
        token_rows, lax.all_gather(value_weight, axes, axis=0, tiled=True), preferred_element_type=jnp.float32
    )
    keys = keys.astype(jnp.bfloat16).reshape(local_blocks, BLOCK, KVH, DH)
    values = values.astype(jnp.bfloat16).reshape(local_blocks, BLOCK, KVH, DH)
    packed = jnp.concatenate([keys, values], axis=3).transpose(0, 2, 1, 3)
    edge = lax.ppermute(packed[local_blocks - 1], "seq", [(s, s + 1) for s in range(devices - 1)])
    replies = jnp.take(
        packed.reshape(local_blocks * KVH, BLOCK, 2 * DH), jnp.maximum(wanted - 1, 0), axis=0, mode="clip"
    )
    arrived = lax.all_to_all(replies, "seq", split_axis=0, concat_axis=0, tiled=True)
    table = jnp.concatenate([target_dev, lax.axis_index("seq")[None]]).astype(jnp.int32)
    return attend(table, queries[0], packed, edge, arrived)[None]


def solution(mesh):
    placed = (
        P("fsdp", "seq", None),
        P("fsdp", "seq", None),
        P(("fsdp", "seq"), None),
        P(("fsdp", "seq"), None),
        P("fsdp", None, "seq"),
    )
    return jax.shard_map(
        local, mesh=mesh, in_specs=placed, out_specs=P("fsdp", "seq", None), check_vma=False
    )
```

time: 1170 us -> 390 us (0.33)
  waiting for transfers between devices: 864 us -> 306 us
  starting transfers between devices: 117 us -> 10.6 us
  other arithmetic: 66 us -> 1.89 us
  local copies, waits for them, and re-layouts: 66.5 us -> 5.12 us
  blocking collectives: 0 us -> 22.3 us
  matrix products: 28.5 us -> 11.4 us
  Pallas kernels: 0 us -> 16.2 us
    all_to_all x16 -> x1, waiting for transfers between devices: 695 us -> 75.3 us  [local(): lax.all_to_all(replies, 'seq', split_axis=0, concat_axis=0, tiled=True)]
    all_to_all x16 -> x1, starting transfers between devices: 113 us -> 7.07 us  [local(): lax.all_to_all(replies, 'seq', split_axis=0, concat_axis=0, tiled=True)]
    all_gather x2, waiting for transfers between devices: 168 us -> 214 us  [the longest x1 113 us: local(): lax.all_gather(value_weight, axes, axis=0, tiled=True)]
    gather x16 -> x1, local copies, waits for them, and re-layouts: 46.1 us -> 2.8 us  [local(): jnp.take(packed.reshape(local_blocks * KVH, BLOCK, 2 * DH), jnp.maximum(w...]
    select_n x9 -> x0, other arithmetic: 32.5 us -> none  [the longest x8 31.8 us: fetch_blocks(): jnp.where((wanted > 0)[:, :, None, None], replies, jnp.zeros_like(replies))]
    all_to_all x0 -> x1, blocking collectives: none -> 22.3 us  [local(): lax.all_to_all(requests[:, None], 'seq', split_axis=0, concat_axis=0, til...]
    pallas_call x0 -> x1, Pallas kernels: none -> 16.2 us  [attend(): pl.pallas_call(attend_kernel, out_shape=jax.ShapeDtypeStruct((rows, width...]
    ppermute x1, waiting for transfers between devices: 0.01 us -> 15.5 us  [local(): lax.ppermute(packed[local_blocks - 1], 'seq', [(s, s + 1) for s in range(...]
  transfers between devices with their start and end apart: 19 -> 4, of which waited for: 15 -> 4; matrix products, arithmetic and copies ran while one was open for 12% -> 2% of each run, Pallas kernels for 0% -> 0%
where the time goes in v1:
time: 390 us; the launch traced here: 387 us
  waiting for transfers between devices  306 us (78%)
  blocking collectives  22.3 us (6%)
  Pallas kernels  16.2 us (4%)
  between operations  13.5 us (3%)
  matrix products  11.4 us (3%)
  starting transfers between devices  10.6 us (3%)
  local copies, waits for them, and re-layouts  5.12 us (1%)
    all_gather x1, waiting for transfers between devices, local(): lax.all_gather(value_weight, axes, axis=0, tiled=True)  113 us
    all_gather x1, waiting for transfers between devices, local(): lax.all_gather(key_weight, axes, axis=0, tiled=True)  101 us
    all_to_all x1, waiting for transfers between devices, local(): lax.all_to_all(replies, 'seq', split_axis=0, concat_axis=0, tiled=True)  75.3 us
    all_to_all x1, blocking collectives, local(): lax.all_to_all(requests[:, None], 'seq', split_axis=0, concat_axis=0, til...  22.3 us
    pallas_call x1, Pallas kernels, attend(): pl.pallas_call(attend_kernel, out_shape=jax.ShapeDtypeStruct((rows, width...  16.2 us
    ppermute x1, waiting for transfers between devices, local(): lax.ppermute(packed[local_blocks - 1], 'seq', [(s, s + 1) for s in range(...  15.5 us
  transfers between devices with their start and end apart: 4, of which 4 were waited for; matrix products, arithmetic and copies ran while one was open for 2% of the time, Pallas kernels for 0%

profile of v1, /device:TPU:1, one launch (start us, length us, event | category | flops | bytes accessed | tf_op | source)
XLA Modules:
  0.0 387.1 jit_solution(9932537446407512925)
XLA Ops:
  6.5 0.7 all-gather.3.cloned.1.call-update
  7.3 0.7 all-gather.5.cloned.1.call-update
  8.1 0.8 copy.18
  8.9 0.1 squeeze.13
  9.0 0.1 select_reduce_fusion
  9.0 0.1 copy.21
  9.1 22.3 %all_to_all.14 = s32[64,1,1]{2,1,0:T(1,128)S(1)} all-to-all(s32[64,1,1]{2,1,0:T(1,128)S(1)} %copy.21), channel_id=1, replica_groups=mesh['fsdp'=4,'seq'=64] {'seq'}, dimensions={0} | all-to-all | bytes 512 | tf_op jit(solution)/shard_map/all_to_all | solution.py:69
  31.5 1.2 maximum_reduce_fusion
  32.7 100.9 %all-gather.3.cloned.1.call-done = bf16[4096,1024]{1,0:T(8,128)(2,1)} async-done(((bf16[16,1024]{1,0:T(8,128)(2,1)}), bf16[4096,1024]{1,0:T(8,128)(2,1)}) %all-gather.3.cloned.1.call-update) | async-done | bytes 8388624 | tf_op jit(solution)/shard_map/all_gather | solution.py:71
  133.6 5.7 %fusion.13 = bf16[32,8,8,128]{3,1,2,0:T(8,128)(2,1)S(1)} fusion(bf16[4096,1024]{1,0:T(8,128)(2,1)} %all-gather.3.cloned.1.call-done, bf16[1,256,4096]{2,1,0:T(8,128)(2,1)S(1)} %copy-done), kind=kOutput, calls=%fused_computation.8 | convolution fusion | flops 2147745792 | bytes 11010048 | tf_op jit(solution)/shard_map/dot_general | solution.py:70
  139.3 0.1 copy.22
  139.4 0.1 copy_dynamic-update-slice_fusion.1
  139.5 112.8 %all-gather.5.cloned.1.call-done = bf16[4096,1024]{1,0:T(8,128)(2,1)} async-done(((bf16[16,1024]{1,0:T(8,128)(2,1)}), bf16[4096,1024]{1,0:T(8,128)(2,1)}) %all-gather.5.cloned.1.call-update) | async-done | bytes 8388624 | tf_op jit(solution)/shard_map/all_gather | solution.py:74
  252.4 5.7 %fusion.10 = bf16[32,8,8,128]{3,1,2,0:T(8,128)(2,1)S(1)} fusion(bf16[4096,1024]{1,0:T(8,128)(2,1)} %all-gather.5.cloned.1.call-done, bf16[1,256,4096]{2,1,0:T(8,128)(2,1)S(1)} %copy-done), kind=kOutput, calls=%fused_computation.7 | convolution fusion | flops 2147745792 | bytes 11010048 | tf_op jit(solution)/shard_map/dot_general | solution.py:73
  258.1 0.1 copy.23
  258.2 0.2 copy_dynamic-update-slice_fusion
  258.4 2.8 gather_fusion
  261.2 7.1 %all-to-all-start.1 = ((bf16[64,128,256]{2,1,0:T(8,128)(2,1)}), bf16[64,128,256]{2,1,0:T(8,128)(2,1)}, u32[]{:S(2)}, u32[]{:S(2)}) async-start(bf16[64,128,256]{2,1,0:T(8,128)(2,1)} %gather_fusion), calls=%async_computation.1 | async-start | bytes 8388608 | tf_op jit(solution)/shard_map/all_to_all | solution.py:83
  268.3 0.8 slice_bitcast_fusion
  269.1 3.5 collective-permute-start
  272.6 0.6 pad_add_fusion.table_ref
  273.2 15.5 %collective-permute-done.edge_ref = bf16[8,128,256]{2,1,0:T(8,128)(2,1)S(1)} collective-permute-done((bf16[8,128,256]{2,1,0:T(8,128)(2,1)}, bf16[8,128,256]{2,1,0:T(8,128)(2,1)S(1)}, u32[]{:S(2)}, u32[]{:S(2)}) %collective-permute-start) | collective-permute-done | bytes 524320 | tf_op jit(solution)/shard_map/ppermute | solution.py:79
  288.7 75.3 %all-to-all-done.1.sorted_ref = bf16[64,128,256]{2,1,0:T(8,128)(2,1)} async-done(((bf16[64,128,256]{2,1,0:T(8,128)(2,1)}), bf16[64,128,256]{2,1,0:T(8,128)(2,1)}, u32[]{:S(2)}, u32[]{:S(2)}) %all-to-all-start.1) | async-done | bytes 4194336 | tf_op jit(solution)/shard_map/all_to_all | solution.py:83
  364.0 16.2 %attend.1 = bf16[256,4096]{1,0:T(8,128)(2,1)} custom-call(s32[17]{0:T(128)} %pad_add_fusion.table_ref, bf16[256,4096]{1,0:T(8,128)(2,1)} %bitcast.38, bf16[2,8,128,256]{3,2,1,0:T(8,128)(2,1)} %bitcast.34, bf16[2,8,128,256]{3,2,1,0:T(8,128)(2,1)} %bitcast.35, bf16[8,128,256]{2,1,0:T(8,128)(2,1)} %copy-done.2, bf16[64,128,256]{2,1,0:T(8,128)(2,1)} %all-to-all-done.1.sorted_ref), custom_call_target="tpu_custom_call" | custom-call | tf_op jit(solution)/shard_map/attend/pallas_call | solution.py:40
  (12 shorter events, 0.2 us)
Async XLA Ops:
  6.5 127.1 %copy-start = (bf16[1,256,4096]{2,1,0:T(8,128)(2,1)S(1)}, bf16[1,256,4096]{2,1,0:T(8,128)(2,1)}, u32[]{:S(2)}) copy-start(bf16[1,256,4096]{2,1,0:T(8,128)(2,1)} %param.5) | copy-start | bytes 6291460
  6.5 127.1 %all-gather.3.cloned.1.call-start = ((), (), s32[]{:S(2)}) async-start(), calls=%async_computation.2 | async-start | bytes 8421376 | tf_op jit(solution)/shard_map/all_gather | solution.py:71
  7.3 245.1 %all-gather.5.cloned.1.call-start = ((), (), s32[]{:S(2)}) async-start(), calls=%async_computation.3 | async-start | bytes 8421376 | tf_op jit(solution)/shard_map/all_gather | solution.py:74
  258.4 9.9 %copy-start.1 = (bf16[2,128,8,256]{3,1,2,0:T(8,128)(2,1)}, bf16[2,128,8,256]{3,1,2,0:T(8,128)(2,1)S(1)}, u32[]{:S(2)}) copy-start(bf16[2,128,8,256]{3,1,2,0:T(8,128)(2,1)S(1)} %copy_dynamic-update-slice_fusion) | copy-start | bytes 3145732
  261.2 102.8 %all-to-all-start.1 = ((bf16[64,128,256]{2,1,0:T(8,128)(2,1)}), bf16[64,128,256]{2,1,0:T(8,128)(2,1)}, u32[]{:S(2)}, u32[]{:S(2)}) async-start(bf16[64,128,256]{2,1,0:T(8,128)(2,1)} %gather_fusion), calls=%async_computation.1 | async-start | bytes 8388608 | tf_op jit(solution)/shard_map/all_to_all | solution.py:83
  269.1 19.6 %collective-permute-start = (bf16[8,128,256]{2,1,0:T(8,128)(2,1)}, bf16[8,128,256]{2,1,0:T(8,128)(2,1)S(1)}, u32[]{:S(2)}, u32[]{:S(2)}) collective-permute-start(bf16[8,128,256]{2,1,0:T(8,128)(2,1)} %slice_bitcast_fusion), channel_id=1, source_target_pairs={{0,1},{1,2},{2,3},{3,4},{4,5},{5,6},{6,7},{7,8},{8,9},{9,10},{10,1... | collective-permute-start | bytes 1572872 | tf_op jit(solution)/shard_map/ppermute | solution.py:79
  288.6 75.3 %copy-start.2 = (bf16[8,128,256]{2,1,0:T(8,128)(2,1)}, bf16[8,128,256]{2,1,0:T(8,128)(2,1)S(1)}, u32[]{:S(2)}) copy-start(bf16[8,128,256]{2,1,0:T(8,128)(2,1)S(1)} %collective-permute-done.edge_ref) | copy-start | bytes 1572868
Sparse Core Ops, SparseCore 0:
  11.1 122.4 all-gather.2
  137.3 115.0 all-gather.4

commit v2 on v1

--- a/solution.py
+++ b/solution.py
@@ -12,6 +12,200 @@
 KVH = 8
 GROUP = 4
 BLOCK = 128
+
+
+MESH = pl.DeviceIdType.MESH
+AXES = ("x", "z", "y")
+
+
+class Place:
+    def __init__(self, sizes):
+        self.sizes = sizes
+        seq = lax.axis_index("seq")
+        self.core = lax.rem(seq, 2)
+        pair = lax.div(seq, 2)
+        self.at = {"x": lax.axis_index("fsdp"), "y": lax.rem(pair, sizes["y"]), "z": lax.div(pair, sizes["y"])}
+
+    def moved(self, axis, steps):
+        return lax.rem(self.at[axis] + (steps % self.sizes[axis]), self.sizes[axis])
+
+    def device(self, axis, steps):
+        at = dict(self.at)
+        at[axis] = self.moved(axis, steps)
+        return (at["x"], (at["z"] * self.sizes["y"] + at["y"]) * 2 + self.core)
+
+    def sibling(self):
+        return (self.at["x"], (self.at["z"] * self.sizes["y"] + self.at["y"]) * 2 + 1 - self.core)
+
+
+class Copies:
+    def __init__(self, send_sem, recv_sem):
+        self.send_sem, self.recv_sem = send_sem, recv_sem
+        self.started = []
+
+    def start(self, ref, device):
+        slot = len(self.started)
+        copy = pltpu.make_async_remote_copy(
+            src_ref=ref, dst_ref=ref, send_sem=self.send_sem.at[slot], recv_sem=self.recv_sem.at[slot],
+            device_id=device, device_id_type=MESH,
+        )
+        copy.start()
+        self.started.append(copy)
+        return slot, device
+
+    def arrived(self, ticket, ref):
+        slot, device = ticket
+        pltpu.make_async_remote_copy(
+            src_ref=ref, dst_ref=ref, send_sem=self.send_sem.at[slot], recv_sem=self.recv_sem.at[slot],
+            device_id=device, device_id_type=MESH,
+        ).wait_recv()
+
+    def sent(self):
+        for copy in self.started:
+            copy.wait_send()
+
+
+def run_tasks(tasks):
+    queue = [[0.0, index, task] for index, task in enumerate(tasks)]
+    while queue:
+        queue.sort(key=lambda entry: entry[:2])
+        entry = queue[0]
+        try:
+            wake, more = next(entry[2])
+            entry[0] = wake
+            for task in more:
+                queue.append([wake, len(queue) + 1000, task])
+        except StopIteration:
+            queue.pop(0)
+
+
+def gather_tasks(place, copies, gathered, part, order, width, handed):
+    full = slice(None)
+
+    def piece(where, half=None, core=None):
+        cols = full if half is None else pl.ds(half * (width // 2), width // 2)
+        at = [where[axis] for axis in AXES]
+        return gathered.at[part, at[0], at[1], at[2], place.core if core is None else core, :, cols]
+
+    def hand_over(where):
+        ticket = copies.start(piece(where), place.sibling())
+        handed.append((ticket, piece(where, core=1 - place.core)))
+
+    def ring(axis, where, begin, span, on_arrival):
+        half_way = place.sizes[axis] // 2
+        ahead = copies.start(piece({**where, axis: place.at[axis]}), place.device(axis, 1))
+        behind = copies.start(piece({**where, axis: place.at[axis]}), place.device(axis, -1))
+        for step in range(1, half_way + 1):
+            last = step == half_way
+            before = {**where, axis: place.moved(axis, -step)}
+            after = {**where, axis: place.moved(axis, step)}
+            yield begin + step * span, []
+            copies.arrived(ahead, piece(before, 0 if last else None))
+            if not last:
+                split = step + 1 == half_way
+                ahead = copies.start(piece(before, 0 if split else None), place.device(axis, 1))
+            copies.arrived(behind, piece(after, 1 if last else None))
+            if not last:
+                behind = copies.start(piece(after, 1 if split else None), place.device(axis, -1))
+            for here in [after] if last else [before, after]:
+                yield begin + step * span, on_arrival(here, begin + step * span)
+
+    first, second, third = order
+
+    def third_ring(where, begin):
+        def on_arrival(here, time):
+            hand_over(here)
+            return []
+
+        return ring(third, where, begin, 10.0, on_arrival)
+
+    def spread(where, time):
+        hand_over(where)
+        return [third_ring({**where, third: full_at(third)}, time)]
+
+    def full_at(axis):
+        return place.at[axis]
+
+    def whole():
+        yield from ring(first, dict(place.at), 0.0, 2.0, lambda here, time: [])
+        slab = {**place.at, first: full}
+        yield 8.0, [ring(second, slab, 8.0, 8.0, spread)]
+        hand_over(slab)
+        yield 8.1, [third_ring(slab, 8.1)]
+
+    return whole()
+
+
+def project_kernel(sizes, tokens_ref, key_ref, value_ref, out_ref, gathered, rows, load_sem, send_sem, recv_sem):
+    place = Place(sizes)
+    width = key_ref.shape[1]
+    at = [place.at[axis] for axis in AXES]
+    loads = [
+        pltpu.make_async_copy(ref, gathered.at[part, at[0], at[1], at[2], place.core], load_sem.at[part])
+        for part, ref in enumerate((key_ref, value_ref))
+    ]
+    loads.append(pltpu.make_async_copy(tokens_ref, rows, load_sem.at[2]))
+    for load in loads:
+        load.start()
+    barrier = pltpu.get_barrier_semaphore()
+    neighbours = [place.device(axis, step) for axis in AXES for step in (1, -1)] + [place.sibling()]
+    for device in neighbours:
+        pl.semaphore_signal(barrier, inc=1, device_id=device, device_id_type=MESH)
+    pl.semaphore_wait(barrier, len(neighbours))
+    loads[0].wait()
+    loads[1].wait()
+    copies = Copies(send_sem, recv_sem)
+    handed = []
+    run_tasks([
+        gather_tasks(place, copies, gathered, 0, ("z", "y", "x"), width, handed),
+        gather_tasks(place, copies, gathered, 1, ("z", "x", "y"), width, handed),
+    ])
+    for ticket, ref in handed:
+        copies.arrived(ticket, ref)
+    loads[2].wait()
+    depth = rows.shape[1]
+    tile = 2 * DH
+
+    def column_tile(step, carry):
+        part = lax.div(step, width // tile)
+        column = lax.rem(step, width // tile)
+        cols = pl.ds(pl.multiple_of(column * tile, tile), tile)
+        weight = gathered[part, :, :, :, :, :, cols].reshape(depth, tile)
+        result = jnp.dot(rows[...], weight, preferred_element_type=jnp.float32).astype(jnp.bfloat16)
+        lanes = pl.ds(pl.multiple_of(part * DH, DH), DH)
+        for block in range(rows.shape[0] // BLOCK):
+            for head in range(2):
+                out_ref[block, column * 2 + head, :, lanes] = result[
+                    block * BLOCK : (block + 1) * BLOCK, head * DH : (head + 1) * DH
+                ]
+        return carry
+
+    lax.fori_loop(0, 2 * (width // tile), column_tile, 0)
+    copies.sent()
+
+
+def project(token_rows, key_weight, value_weight, sizes):
+    local_tokens, depth = token_rows.shape
+    part_rows, width = key_weight.shape
+    blocks = local_tokens // BLOCK
+    hbm = pl.BlockSpec(memory_space=pltpu.HBM)
+    return pl.pallas_call(
+        functools.partial(project_kernel, sizes),
+        out_shape=jax.ShapeDtypeStruct((blocks, KVH, BLOCK, 2 * DH), jnp.bfloat16),
+        in_specs=[hbm] * 3,
+        out_specs=pl.BlockSpec(memory_space=pltpu.VMEM),
+        scratch_shapes=[
+            pltpu.VMEM((2, sizes["x"], sizes["z"], sizes["y"], 2, part_rows, width), jnp.bfloat16),
+            pltpu.VMEM((local_tokens, depth), jnp.bfloat16),
+            pltpu.SemaphoreType.DMA((3,)),
+            pltpu.SemaphoreType.DMA((88,)),
+            pltpu.SemaphoreType.DMA((88,)),
+        ],
+        compiler_params=pltpu.CompilerParams(
+            collective_id=0, has_side_effects=True, vmem_limit_bytes=48 << 20
+        ),
+        name="project",
+    )(token_rows, key_weight, value_weight)
 
 
 def attend_kernel(table_ref, q_ref, own_ref, first_ref, edge_ref, sorted_ref, out_ref):
@@ -60,22 +254,14 @@
     token_rows = tokens[0]
     local_blocks = token_rows.shape[0] // BLOCK
     devices = lax.axis_size("seq")
-    axes = ("fsdp", "seq")
     targets = sorted_blocks[0]
     target_dev = (targets // local_blocks).reshape(-1)
     item = (targets % local_blocks) * KVH + jnp.arange(KVH, dtype=jnp.int32)[:, None]
     hit = target_dev[:, None] == jnp.arange(devices, dtype=jnp.int32)[None, :]
     requests = jnp.sum(jnp.where(hit, (item.reshape(-1) + 1)[:, None], 0), axis=0)
     wanted = lax.all_to_all(requests[:, None], "seq", split_axis=0, concat_axis=0, tiled=True)[:, 0]
-    keys = jnp.dot(
-        token_rows, lax.all_gather(key_weight, axes, axis=0, tiled=True), preferred_element_type=jnp.float32
-    )
-    values = jnp.dot(
-        token_rows, lax.all_gather(value_weight, axes, axis=0, tiled=True), preferred_element_type=jnp.float32
-    )
-    keys = keys.astype(jnp.bfloat16).reshape(local_blocks, BLOCK, KVH, DH)
-    values = values.astype(jnp.bfloat16).reshape(local_blocks, BLOCK, KVH, DH)
-    packed = jnp.concatenate([keys, values], axis=3).transpose(0, 2, 1, 3)
+    sizes = {"x": lax.axis_size("fsdp"), "y": 4, "z": devices // 8}
+    packed = project(token_rows, key_weight, value_weight, sizes)
     edge = lax.ppermute(packed[local_blocks - 1], "seq", [(s, s + 1) for s in range(devices - 1)])
     replies = jnp.take(
         packed.reshape(local_blocks * KVH, BLOCK, 2 * DH), jnp.maximum(wanted - 1, 0), axis=0, mode="clip"

time: 390 us -> 214 us (0.55)
  waiting for transfers between devices: 306 us -> 91.5 us
  Pallas kernels: 16.2 us -> 86.8 us
  blocking collectives: 22.3 us -> 0 us
  between operations: 13.5 us -> 0.09 us
  starting transfers between devices: 10.6 us -> 23.2 us
  matrix products: 11.4 us -> 0 us
    all_gather x2 -> x0, waiting for transfers between devices: 214 us -> none  [the longest x1 113 us: local(): lax.all_gather(value_weight, axes, axis=0, tiled=True)]
    pallas_call x0 -> x1, Pallas kernels: none -> 70.6 us  [project(): pl.pallas_call(functools.partial(project_kernel, sizes), out_shape=jax.Sh...]
    all_to_all x1 -> x0, blocking collectives: 22.3 us -> none  [local(): lax.all_to_all(requests[:, None], 'seq', split_axis=0, concat_axis=0, til...]
    all_to_all x0 -> x1, starting transfers between devices: none -> 13.2 us  [local(): lax.all_to_all(requests[:, None], 'seq', split_axis=0, concat_axis=0, til...]
    dot_general x2 -> x0, matrix products: 11.4 us -> none  [the longest x1 5.71 us: local(): jnp.dot(token_rows, lax.all_gather(key_weight, axes, axis=0, tiled=True),...]
  transfers between devices with their start and end apart: 4 -> 3, of which waited for: 4 -> 2; matrix products, arithmetic and copies ran while one was open for 2% -> 0% of each run, Pallas kernels for 0% -> 33%
where the time goes in v2:
time: 214 us; the launch traced here: 211 us
  waiting for transfers between devices  91.5 us (43%)
  Pallas kernels  86.8 us (41%)
  starting transfers between devices  23.2 us (11%)
  local copies, waits for them, and re-layouts  7.58 us (4%)
    all_to_all x1, waiting for transfers between devices, local(): lax.all_to_all(replies, 'seq', split_axis=0, concat_axis=0, tiled=True)  75.4 us
    pallas_call x1, Pallas kernels, project(): pl.pallas_call(functools.partial(project_kernel, sizes), out_shape=jax.Sh...  70.6 us
    pallas_call x1, Pallas kernels, attend(): pl.pallas_call(attend_kernel, out_shape=jax.ShapeDtypeStruct((rows, width...  16.2 us
    ppermute x1, waiting for transfers between devices, local(): lax.ppermute(packed[local_blocks - 1], 'seq', [(s, s + 1) for s in range(...  16.1 us
    all_to_all x1, starting transfers between devices, local(): lax.all_to_all(requests[:, None], 'seq', split_axis=0, concat_axis=0, til...  13.2 us
    all_to_all x1, starting transfers between devices, local(): lax.all_to_all(replies, 'seq', split_axis=0, concat_axis=0, tiled=True)  6.48 us
  transfers between devices with their start and end apart: 3, of which 2 were waited for; matrix products, arithmetic and copies ran while one was open for 0% of the time, Pallas kernels for 33%

profile of v2, /device:TPU:1, one launch (start us, length us, event | category | flops | bytes accessed | tf_op | source)
XLA Modules:
  0.0 211.1 jit_solution(12139186622999146800)
XLA Ops:
  0.0 0.1 add.50
  0.1 0.8 copy.12
  0.8 0.1 squeeze.13
  0.9 0.1 select_reduce_fusion
  1.0 0.7 copy.13
  1.7 13.2 %all-to-all-start = ((s32[64,1,1]{2,1,0:T(1,128)}), s32[64,1,1]{2,1,0:T(1,128)S(1)}, u32[]{:S(2)}, u32[]{:S(2)}) async-start(s32[64,1,1]{2,1,0:T(1,128)} %copy.13), calls=%async_computation | async-start | bytes 65536 | tf_op jit(solution)/shard_map/all_to_all | solution.py:262
  14.9 0.0 copy-start.1
  14.9 1.6 copy-done.1
  16.5 0.0 copy-start.2
  16.5 0.8 copy-done.2
  17.3 0.8 copy-done.3
  18.0 70.6 %project.1.own_ref.first_ref = bf16[2,8,128,256]{3,2,1,0:T(8,128)(2,1)S(1)} custom-call(bf16[256,4096]{1,0:T(8,128)(2,1)S(1)} %bitcast.9, bf16[16,1024]{1,0:T(8,128)(2,1)S(1)} %copy-done.2, bf16[16,1024]{1,0:T(8,128)(2,1)S(1)} %copy-done.3), custom_call_target="tpu_custom_call" | custom-call | tf_op jit(solution)/shard_map/project/pallas_call | solution.py:192
  88.6 0.0 copy-start
  88.6 0.0 all-to-all-done
  88.6 1.2 maximum_reduce_fusion
  89.9 2.8 %gather_fusion = bf16[64,128,256]{2,1,0:T(8,128)(2,1)} fusion(bf16[16,128,256]{2,1,0:T(8,128)(2,1)S(1)} %bitcast.8, s32[1024]{0:T(1024)S(1)} %pad_clamp_fusion), kind=kCustom, calls=%fused_computation | custom fusion | bytes 8388864 | tf_op jit(solution)/shard_map/jit(_take)/gather | solution.py:266
  92.7 6.5 %all-to-all-start.1 = ((bf16[64,128,256]{2,1,0:T(8,128)(2,1)}), bf16[64,128,256]{2,1,0:T(8,128)(2,1)}, u32[]{:S(2)}, u32[]{:S(2)}) async-start(bf16[64,128,256]{2,1,0:T(8,128)(2,1)} %gather_fusion), calls=%async_computation.1 | async-start | bytes 8388608 | tf_op jit(solution)/shard_map/all_to_all | solution.py:269
  99.1 0.0 copy-done
  99.2 3.5 %collective-permute-start = (bf16[8,128,256]{2,1,0:T(8,128)(2,1)S(1)}, bf16[8,128,256]{2,1,0:T(8,128)(2,1)S(1)}, u32[]{:S(2)}, u32[]{:S(2)}) collective-permute-start(bf16[8,128,256]{2,1,0:T(8,128)(2,1)S(1)} %slice_bitcast_fusion), channel_id=1, source_target_pairs={{0,1},{1,2},{2,3},{3,4},{4,5},{5,6},{6,7},{7,8},{8,9},{9,10},{10,1... | collective-permute-start | bytes 1572872 | tf_op jit(solution)/shard_map/ppermute | solution.py:265
  102.7 0.6 pad_add_fusion.table_ref
  103.3 16.1 %collective-permute-done.edge_ref = bf16[8,128,256]{2,1,0:T(8,128)(2,1)S(1)} collective-permute-done((bf16[8,128,256]{2,1,0:T(8,128)(2,1)S(1)}, bf16[8,128,256]{2,1,0:T(8,128)(2,1)S(1)}, u32[]{:S(2)}, u32[]{:S(2)}) %collective-permute-start) | collective-permute-done | bytes 524320 | tf_op jit(solution)/shard_map/ppermute | solution.py:265
  119.4 75.4 %all-to-all-done.1.sorted_ref = bf16[64,128,256]{2,1,0:T(8,128)(2,1)} async-done(((bf16[64,128,256]{2,1,0:T(8,128)(2,1)}), bf16[64,128,256]{2,1,0:T(8,128)(2,1)}, u32[]{:S(2)}, u32[]{:S(2)}) %all-to-all-start.1) | async-done | bytes 4194336 | tf_op jit(solution)/shard_map/all_to_all | solution.py:269
  194.9 0.0 copy-done.4
  194.9 16.2 %attend.1 = bf16[256,4096]{1,0:T(8,128)(2,1)} custom-call(s32[17]{0:T(128)} %pad_add_fusion.table_ref, bf16[256,4096]{1,0:T(8,128)(2,1)} %bitcast.10, bf16[2,8,128,256]{3,2,1,0:T(8,128)(2,1)} %copy-done, bf16[2,8,128,256]{3,2,1,0:T(8,128)(2,1)} %copy-done, bf16[8,128,256]{2,1,0:T(8,128)(2,1)} %copy-done.4, bf16[64,128,256]{2,1,0:T(8,128)(2,1)} %all-to-all-done.1.sorted_ref), custom_call_target="tpu_custom_call" | custom-call | tf_op jit(solution)/shard_map/attend/pallas_call | solution.py:234
  (6 shorter events, 0.1 us)
Async XLA Ops:
  1.7 86.9 %all-to-all-start = ((s32[64,1,1]{2,1,0:T(1,128)}), s32[64,1,1]{2,1,0:T(1,128)S(1)}, u32[]{:S(2)}, u32[]{:S(2)}) async-start(s32[64,1,1]{2,1,0:T(1,128)} %copy.13), calls=%async_computation | async-start | bytes 65536 | tf_op jit(solution)/shard_map/all_to_all | solution.py:262
  14.9 1.6 copy-start.1
  16.5 0.8 copy-start.2
  17.3 0.8 copy-start.3
  88.6 10.5 %copy-start = (bf16[2,8,128,256]{3,2,1,0:T(8,128)(2,1)}, bf16[2,8,128,256]{3,2,1,0:T(8,128)(2,1)S(1)}, u32[]{:S(2)}) copy-start(bf16[2,8,128,256]{3,2,1,0:T(8,128)(2,1)S(1)} %project.1.own_ref.first_ref) | copy-start | bytes 3145732
  92.7 102.2 %all-to-all-start.1 = ((bf16[64,128,256]{2,1,0:T(8,128)(2,1)}), bf16[64,128,256]{2,1,0:T(8,128)(2,1)}, u32[]{:S(2)}, u32[]{:S(2)}) async-start(bf16[64,128,256]{2,1,0:T(8,128)(2,1)} %gather_fusion), calls=%async_computation.1 | async-start | bytes 8388608 | tf_op jit(solution)/shard_map/all_to_all | solution.py:269
  99.2 20.2 %collective-permute-start = (bf16[8,128,256]{2,1,0:T(8,128)(2,1)S(1)}, bf16[8,128,256]{2,1,0:T(8,128)(2,1)S(1)}, u32[]{:S(2)}, u32[]{:S(2)}) collective-permute-start(bf16[8,128,256]{2,1,0:T(8,128)(2,1)S(1)} %slice_bitcast_fusion), channel_id=1, source_target_pairs={{0,1},{1,2},{2,3},{3,4},{4,5},{5,6},{6,7},{7,8},{8,9},{9,10},{10,1... | collective-permute-start | bytes 1572872 | tf_op jit(solution)/shard_map/ppermute | solution.py:265
  119.4 75.4 %copy-start.4 = (bf16[8,128,256]{2,1,0:T(8,128)(2,1)}, bf16[8,128,256]{2,1,0:T(8,128)(2,1)S(1)}, u32[]{:S(2)}) copy-start(bf16[8,128,256]{2,1,0:T(8,128)(2,1)S(1)} %collective-permute-done.edge_ref) | copy-start | bytes 1572868

commit v3 on v1

v3 whole, which is shorter than its diff:
```python
import functools
import math

import jax
import jax.numpy as jnp
from jax import lax
from jax.experimental import pallas as pl
from jax.experimental.pallas import tpu as pltpu
from jax.sharding import PartitionSpec as P

DH = 128
KVH = 8
GROUP = 4
BLOCK = 128
MESH = pl.DeviceIdType.MESH
AXES = ("x", "z", "y")
FULL = slice(None)
LANES = 128
STAGES = ((0, 3), (3, 5), (5, 7), (7, 8))


class Place:
    def __init__(self, sizes):
        self.sizes = sizes
        self.seq = lax.axis_index("seq")
        self.core = lax.rem(self.seq, 2)
        pair = lax.div(self.seq, 2)
        self.at = {"x": lax.axis_index("fsdp"), "y": lax.rem(pair, sizes["y"]), "z": lax.div(pair, sizes["y"])}
        self.columns = 2 * sizes["y"]
        self.column = self.at["y"] * 2 + self.core

    def moved(self, axis, steps):
        return lax.rem(self.at[axis] + (steps % self.sizes[axis]), self.sizes[axis])

    def device(self, axis, steps):
        at = dict(self.at)
        at[axis] = self.moved(axis, steps)
        return (at["x"], (at["z"] * self.sizes["y"] + at["y"]) * 2 + self.core)

    def sibling(self):
        return (self.at["x"], self.at["z"] * self.columns + self.at["y"] * 2 + 1 - self.core)

    def other_column(self, steps):
        return lax.rem(self.column + (steps % self.columns), self.columns)

    def in_row(self, steps):
        return (self.at["x"], self.at["z"] * self.columns + self.other_column(steps))

    def along(self, steps):
        count = self.sizes["z"] * self.columns
        return (self.at["x"], lax.rem(self.seq + (steps % count), count))


class Copies:
    def __init__(self, send_sem, recv_sem):
        self.send_sem, self.recv_sem = send_sem, recv_sem
        self.started = []

    def make(self, slot, source, target, device):
        return pltpu.make_async_remote_copy(
            src_ref=source, dst_ref=target, send_sem=self.send_sem.at[slot], recv_sem=self.recv_sem.at[slot],
            device_id=device, device_id_type=MESH,
        )

    def start(self, source, target, device):
        slot = len(self.started)
        copy = self.make(slot, source, target, device)
        copy.start()
        self.started.append(copy)
        return slot, device

    def arrived(self, ticket, target):
        self.make(ticket[0], target, target, ticket[1]).wait_recv()

    def sent(self):
        for copy in self.started:
            copy.wait_send()


def run_tasks(tasks):
    count = 0
    queue = []
    for task in tasks:
        queue.append([0.0, count, task])
        count += 1
    while queue:
        queue.sort(key=lambda entry: entry[:2])
        entry = queue[0]
        try:
            wake, more = next(entry[2])
            entry[0] = wake
            for task in more:
                queue.append([wake, count, task])
                count += 1
        except StopIteration:
            queue.pop(0)


class Group:
    def __init__(self, then):
        self.open, self.then = 0, then

    def add(self, task):
        self.open += 1

        def run():
            wake = 0.0
            for wake, more in task:
                yield wake, more
            self.open -= 1
            if self.open == 0:
                yield wake, self.then(wake)

        return run()


def ring(place, copies, piece, axis, where, begin, span, on_arrival, halves=True):
    half_way = place.sizes[axis] // 2
    yield begin, []
    own = piece({**where, axis: place.at[axis]}, None)
    ahead = copies.start(own, own, place.device(axis, 1))
    behind = copies.start(own, own, place.device(axis, -1))
    for step in range(1, half_way + 1):
        last, split = step == half_way, step + 1 == half_way
        before = {**where, axis: place.moved(axis, -step)}
        after = {**where, axis: place.moved(axis, step)}
        time = begin + step * span
        yield time, []
        copies.arrived(ahead, piece(before, 0 if last and halves else None))
        if not last:
            ref = piece(before, 0 if split and halves else None)
            ahead = copies.start(ref, ref, place.device(axis, 1))
        if not last or halves:
            copies.arrived(behind, piece(after, 1 if last else None))
        if not last and not (split and not halves):
            ref = piece(after, 1 if split else None)
            behind = copies.start(ref, ref, place.device(axis, -1))
        for here in [after] if last else [before, after]:
            more = on_arrival(here, time)
            if more:
                yield time, more


def gather_weight(place, copies, group, weights, kind, part, order, ready, begin, spans):
    first, second, third = order

    def piece(where, half):
        rows = FULL if half is None else pl.ds(half * 16, 16)
        at = [where[axis] for axis in AXES]
        return weights.at[kind, part, at[0], at[1], at[2], rows, :]

    def nothing(here, time):
        return []

    def third_ring(where, time):
        return group.add(ring(place, copies, piece, third, {**where, third: place.at[third]}, time, spans[2], nothing))

    def whole():
        yield begin[0], []
        ready(kind, part)
        yield from ring(place, copies, piece, first, dict(place.at), begin[0], spans[0], nothing)
        slab = {**place.at, first: FULL}
        yield begin[1], [
            group.add(ring(place, copies, piece, second, slab, begin[1], spans[1], lambda here, time: [third_ring(here, time)])),
            third_ring(slab, begin[1]),
        ]

    return group.add(whole())


class Kind:
    names = ("own", "back1", "ahead1", "back2", "ahead2", "swap", "edge", "far_out", "far_back", "far_ahead", "last", "slots", "arrived")

    def __init__(self, refs):
        for name, ref in zip(self.names, refs):
            setattr(self, name, ref)

    @classmethod
    def scratch(cls, rows, columns):
        half = KVH // 2
        block = (BLOCK, DH)
        shapes = [(2, KVH)] * 5 + [(2, half), (KVH,), (2, columns + columns // 2)]
        shapes += [(columns + columns // 2,)] * 2 + [(2, columns // 2), (columns - 1, rows), (columns, rows)]
        return [pltpu.VMEM(shape + block, jnp.bfloat16) for shape in shapes]


def layer_kernel(sizes, plan, sorted_ref, list_ref, tokens_ref, queries_ref, key_ref, value_ref, out_ref,
                 weights, tokens, queries, lists, wanted_vector, wanted, softmax, *rest):
    kinds = [Kind(rest[:13]), Kind(rest[13:26])]
    load_sem, send_sem, recv_sem = rest[26:]
    place = Place(sizes)
    copies = Copies(send_sem, recv_sem)
    x, z, y, core = place.at["x"], place.at["z"], place.at["y"], place.core
    columns, rows_z = place.columns, sizes["z"]
    half_width = key_ref.shape[1] // 2
    part_width = half_width // 2

    loads = {}

    def load(name, source, target):
        loads[name] = pltpu.make_async_copy(source, target, load_sem.at[len(loads)])
        loads[name].start()

    def weight_columns(ref, which, part):
        return ref.at[:, pl.ds(pl.multiple_of(which * half_width + part * part_width, part_width), part_width)]

    for kind, ref in enumerate((key_ref, value_ref)):
        for part in range(2):
            load((kind, part), weight_columns(ref, core, part), weights.at[kind, part, x, z, y, pl.ds(core * 16, 16), :])
    load("lists", list_ref, lists.at[z, y, core])
    load("tokens", tokens_ref, tokens.at[core])
    load("queries", queries_ref, queries)

    barrier = pltpu.get_barrier_semaphore()
    peers = [place.device(axis, step) for axis in ("x", "z") for step in (1, -1)]
    peers += [place.in_row(step) for step in range(1, columns)]
    peers += [place.along(1), place.along(-1)]
    for device in peers:
        pl.semaphore_signal(barrier, inc=1, device_id=device, device_id_type=MESH)
    pl.semaphore_wait(barrier, len(peers))

    shared = {}
    for kind, ref in enumerate((key_ref, value_ref)):
        for part in range(2):
            shared[kind, part] = copies.start(
                weight_columns(ref, 1 - core, part), weights.at[kind, part, x, z, y, pl.ds(core * 16, 16), :], place.sibling()
            )
    shared["tokens"] = copies.start(tokens_ref, tokens.at[core], place.sibling())

    def ready(kind, part):
        loads[kind, part].wait()
        copies.arrived(shared[kind, part], weights.at[kind, part, x, z, y, pl.ds((1 - core) * 16, 16), :])

    def list_task():
        def piece(where, half):
            return lists.at[where["z"], where["y"], core]

        def nothing(here, time):
            return []

        loads["lists"].wait()
        yield from ring(place, copies, piece, "z", dict(place.at), 0.0, 2.0, nothing, halves=False)
        yield from ring(place, copies, piece, "y", {**place.at, "z": FULL}, 8.0, 2.0, nothing, halves=False)
        mine = lists.at[:, :, core]
        ticket = copies.start(mine, mine, place.sibling())
        yield 14.5, []
        copies.arrived(ticket, lists.at[:, :, 1 - core])
        lane = lax.broadcasted_iota(jnp.int32, (8, LANES), 1)
        source = lax.broadcasted_iota(jnp.int32, (8, LANES), 0) * columns + place.column

        def one_device(device, total):
            tile = lists[lax.div(device, columns), lax.div(lax.rem(device, columns), 2), lax.rem(device, 2)]
            item = (tile & 1) * KVH + (lane >> 1) + 1
            found = jnp.sum(jnp.where((tile >> 1) == source, item, 0), axis=1, keepdims=True)
            return jnp.where(lane == device, found, total)

        wanted_vector[...] = lax.fori_loop(0, rows_z * columns, one_device, jnp.zeros((8, LANES), jnp.int32))
        copy = pltpu.make_async_copy(wanted_vector, wanted, load_sem.at[len(loads)])
        copy.start()
        copy.wait()

    def picked(ref, steps, row_steps, column):
        device = place.moved("z", row_steps) * columns + column
        item = jnp.clip(wanted[place.moved("z", steps), device] - 1, 0, 2 * KVH - 1)
        return ref[lax.div(item, KVH), lax.rem(item, KVH)]

    def project(kind):
        buffers = kinds[kind]
        if kind == 0:
            loads["tokens"].wait()
            copies.arrived(shared["tokens"], tokens.at[1 - core])
        for part in range(2):
            weight = weights[kind, part].reshape(tokens.shape[2], part_width)
            for mine in (False, True):
                which = core if mine else 1 - core
                result = jnp.dot(tokens[which], weight, preferred_element_type=jnp.float32).astype(jnp.bfloat16)
                for block in range(2):
                    for head in range(2):
                        value = result[block * BLOCK : (block + 1) * BLOCK, head * DH : (head + 1) * DH]
                        if mine:
                            buffers.own[block, core * (KVH // 2) + part * 2 + head] = value
                        else:
                            buffers.swap[block, part * 2 + head] = value
        return copies.start(buffers.swap, buffers.own.at[:, pl.ds(core * (KVH // 2), KVH // 2)], place.sibling())

    def send_slots(buffers, stage, row_tickets):
        begin, end = STAGES[stage]
        sources = {0: (buffers.own, 0), 1: (buffers.back1, -1), 2: (buffers.ahead1, 1), 3: (buffers.back2, -2), 4: (buffers.ahead2, 2)}

        def value(slot, column):
            if slot < 5:
                return picked(*sources[slot], 0, column)
            if slot == 5:
                return buffers.far_back[column]
            if slot == 6:
                return buffers.far_ahead[column]
            return buffers.last[lax.rem(column, 2), lax.div(column, 2)]

        for slot in range(begin, end):
            buffers.arrived[place.column, slot] = value(slot, place.column)
        for step in range(1, columns):
            column = place.other_column(step)
            for slot in range(begin, end):
                buffers.slots[step - 1, slot] = value(slot, column)
            ticket = copies.start(
                buffers.slots.at[step - 1, pl.ds(begin, end - begin)],
                buffers.arrived.at[place.column, pl.ds(begin, end - begin)],
                place.in_row(step),
            )
            row_tickets.append((ticket, buffers.arrived.at[place.other_column(-step), pl.ds(begin, end - begin)]))

    def send_far(buffers, direction):
        ref = buffers.back2 if direction == 1 else buffers.ahead2
        side = 0 if direction == 1 else 1
        for column in range(columns):
            buffers.far_out[side, column] = picked(ref, -2 * direction, direction, column)
        for index in range(columns // 2):
            buffers.far_out[side, columns + index] = picked(ref, -2 * direction, 2 * direction, 2 * index + side)
        target = buffers.far_back if direction == 1 else buffers.far_ahead
        return copies.start(buffers.far_out.at[side], target, place.device("z", direction))

    def exchange(kind, then):
        times = plan["exchange"][kind]

        def task():
            buffers = kinds[kind]
            row_tickets = []
            ticket = project(kind)
            yield times[0], []
            copies.arrived(ticket, buffers.own.at[:, pl.ds((1 - core) * (KVH // 2), KVH // 2)])
            ahead = copies.start(buffers.own, buffers.back1, place.device("z", 1))
            behind = copies.start(buffers.own, buffers.ahead1, place.device("z", -1))
            edge = copies.start(buffers.own.at[1], buffers.edge, place.along(1))
            yield times[1], []
            copies.arrived(ahead, buffers.back1)
            ahead = copies.start(buffers.back1, buffers.back2, place.device("z", 1))
            copies.arrived(behind, buffers.ahead1)
            behind = copies.start(buffers.ahead1, buffers.ahead2, place.device("z", -1))
            send_slots(buffers, 0, row_tickets)
            yield times[2], []
            copies.arrived(ahead, buffers.back2)
            ahead = send_far(buffers, 1)
            copies.arrived(behind, buffers.ahead2)
            behind = send_far(buffers, -1)
            send_slots(buffers, 1, row_tickets)
            yield times[3], []
            tail = pl.ds(columns, columns // 2)
            copies.arrived(ahead, buffers.far_back)
            ahead = copies.start(buffers.far_back.at[tail], buffers.last.at[0], place.device("z", 1))
            copies.arrived(behind, buffers.far_ahead)
            behind = copies.start(buffers.far_ahead.at[tail], buffers.last.at[1], place.device("z", -1))
            send_slots(buffers, 2, row_tickets)
            yield times[4], []
            copies.arrived(ahead, buffers.last.at[0])
            copies.arrived(behind, buffers.last.at[1])
            send_slots(buffers, 3, row_tickets)
            yield times[5], []
            copies.arrived(edge, buffers.edge)
            for ticket, target in row_tickets:
                copies.arrived(ticket, target)
            yield times[5], then

        return [task()]

    def candidates(kind, block, head):
        buffers = kinds[kind]
        device = lax.div(sorted_ref[head, block], 2)
        distance = lax.rem(lax.div(device, columns) - z + rows_z, rows_z)
        slot = jnp.where(
            distance < 4, 2 * distance, jnp.where(distance == 4, 7, 2 * (rows_z - distance) - 1)
        )
        before = buffers.edge[head] if block == 0 else buffers.own[0, head]
        return jnp.concatenate(
            [buffers.own[block, head], before, buffers.arrived[lax.rem(device, columns), slot]], axis=0
        )

    def weights_task(block, head_range, wake):
        def one_head(head, carry):
            rows = slice(block * BLOCK, (block + 1) * BLOCK)
            query = queries[rows, pl.ds(pl.multiple_of(head * GROUP * DH, GROUP * DH), GROUP * DH)]
            query = jnp.concatenate([query[:, g * DH : (g + 1) * DH] for g in range(GROUP)], axis=0)
            scores = lax.dot_general(
                query, candidates(0, block, head), (((1,), (1,)), ((), ())), preferred_element_type=jnp.float32
            ) * (math.log2(math.e) / math.sqrt(DH))
            if block == 0:
                index = lax.broadcasted_iota(jnp.int32, scores.shape, 1)
                blocked = (place.seq == 0) & (index >= BLOCK) & (index < 2 * BLOCK)
                scores = jnp.where(blocked, -1e30, scores)
            raised = jnp.exp2(scores - jnp.max(scores, axis=-1, keepdims=True))
            scale = 1.0 / jnp.sum(raised, axis=-1, keepdims=True)
            softmax[block * KVH + head] = (raised * scale).astype(jnp.bfloat16)
            return carry

        yield wake, []
        if block == 0 and head_range[0] == 0:
            loads["queries"].wait()
        lax.fori_loop(*head_range, one_head, 0)

    def output_task():
        yield plan["output"], []
        for block in range(2):

            def one_head(head, carry, block=block):
                result = jnp.dot(
                    softmax[block * KVH + head], candidates(1, block, head), preferred_element_type=jnp.float32
                ).astype(jnp.bfloat16)
                for g in range(GROUP):
                    lanes = pl.ds(pl.multiple_of((head * GROUP + g) * DH, DH), DH)
                    out_ref[block * BLOCK : (block + 1) * BLOCK, lanes] = result[g * BLOCK : (g + 1) * BLOCK]
                return carry

            lax.fori_loop(0, KVH, one_head, 0)

    half = KVH // 2
    both = Group(lambda wake: [output_task()])
    softmax_tasks = [
        both.add(weights_task(block, (begin, begin + half), plan["softmax"][block * 2 + begin // half]))
        for block in range(2) for begin in (0, half)
    ]
    values_ready = both.add(iter(()))
    groups = [
        Group(lambda wake: exchange(0, softmax_tasks)),
        Group(lambda wake: exchange(1, [values_ready])),
    ]
    tasks = [list_task()]
    for kind in range(2):
        for part, order in enumerate((("z", "y", "x"), ("z", "x", "y"))):
            tasks.append(
                gather_weight(place, copies, groups[kind], weights, kind, part, order, ready, plan["begin"][kind], plan["spans"])
            )
    run_tasks(tasks)
    copies.sent()
    assert len(copies.started) == COPIES, len(copies.started)


PLAN = {
    "begin": ((0.0, 10.0), (0.5, 27.0)),
    "spans": (2.0, 5.0, 8.0),
    "exchange": ((36.0, 48.0, 60.0, 69.0, 73.0, 78.0), (64.0, 82.0, 94.0, 104.0, 108.0, 114.0)),
    "softmax": (78.5, 82.5, 86.0, 95.0),
    "output": 115.0,
}


def layer(sorted_blocks, lists, tokens, queries, key_weight, value_weight, sizes):
    local_tokens, depth = tokens.shape
    part_rows, width = key_weight.shape
    columns, rows = 2 * sizes["y"], sizes["z"]
    hbm = pl.BlockSpec(memory_space=pltpu.HBM)
    kind = Kind.scratch(rows, columns)
    return pl.pallas_call(
        functools.partial(layer_kernel, sizes, PLAN),
        out_shape=jax.ShapeDtypeStruct(queries.shape, jnp.bfloat16),
        in_specs=[pl.BlockSpec(memory_space=pltpu.SMEM)] + [hbm] * 5,
        out_specs=pl.BlockSpec(memory_space=pltpu.VMEM),
        scratch_shapes=[
            pltpu.VMEM((2, 2, sizes["x"], rows, sizes["y"], 2 * part_rows, width // 4), jnp.bfloat16),
            pltpu.VMEM((2, local_tokens, depth), jnp.bfloat16),
            pltpu.VMEM(queries.shape, jnp.bfloat16),
            pltpu.VMEM((rows, sizes["y"], 2, 8, LANES), jnp.int32),
            pltpu.VMEM((8, LANES), jnp.int32),
            pltpu.SMEM((8, LANES), jnp.int32),
            pltpu.VMEM((2 * KVH, GROUP * BLOCK, 3 * BLOCK), jnp.bfloat16),
            *kind,
            *kind,
            pltpu.SemaphoreType.DMA((8,)),
            pltpu.SemaphoreType.DMA((COPIES,)),
            pltpu.SemaphoreType.DMA((COPIES,)),
        ],
        compiler_params=pltpu.CompilerParams(
            collective_id=0, has_side_effects=True, vmem_limit_bytes=58 << 20
        ),
        name="layer",
    )(sorted_blocks, lists, tokens, queries, key_weight, value_weight)


COPIES = 204


def local(tokens, queries, key_weight, value_weight, sorted_blocks):
    devices = lax.axis_size("seq")
    sizes = {"x": lax.axis_size("fsdp"), "y": 4, "z": devices // 8}
    own = sorted_blocks[0].reshape(-1)
    lists = jnp.broadcast_to(jnp.pad(own, (0, LANES - own.shape[0]), constant_values=-1), (8, LANES))
    return layer(sorted_blocks[0], lists, tokens[0], queries[0], key_weight, value_weight, sizes)[None]


def solution(mesh):
    placed = (
        P("fsdp", "seq", None),
        P("fsdp", "seq", None),
        P(("fsdp", "seq"), None),
        P(("fsdp", "seq"), None),
        P("fsdp", None, "seq"),
    )
    return jax.shard_map(
        local, mesh=mesh, in_specs=placed, out_specs=P("fsdp", "seq", None), check_vma=False
    )
```

time: 390 us -> 172 us (0.44)
  waiting for transfers between devices: 306 us -> 0 us
  Pallas kernels: 16.2 us -> 166 us
  blocking collectives: 22.3 us -> 0 us
  between operations: 13.5 us -> 0.01 us
  matrix products: 11.4 us -> 0 us
  starting transfers between devices: 10.6 us -> 0 us
    all_gather x2 -> x0, waiting for transfers between devices: 214 us -> none  [the longest x1 113 us: local(): lax.all_gather(value_weight, axes, axis=0, tiled=True)]
    pallas_call x1, Pallas kernels: 16.2 us -> 166 us  [layer(): pl.pallas_call(functools.partial(layer_kernel, sizes, PLAN), out_shape=ja...]
    all_to_all x1 -> x0, waiting for transfers between devices: 75.3 us -> none  [local(): lax.all_to_all(replies, 'seq', split_axis=0, concat_axis=0, tiled=True)]
    all_to_all x1 -> x0, blocking collectives: 22.3 us -> none  [local(): lax.all_to_all(requests[:, None], 'seq', split_axis=0, concat_axis=0, til...]
    ppermute x1 -> x0, waiting for transfers between devices: 15.5 us -> none  [local(): lax.ppermute(packed[local_blocks - 1], 'seq', [(s, s + 1) for s in range(...]
    dot_general x2 -> x0, matrix products: 11.4 us -> none  [the longest x1 5.71 us: local(): jnp.dot(token_rows, lax.all_gather(key_weight, axes, axis=0, tiled=True),...]
    all_to_all x1 -> x0, starting transfers between devices: 7.07 us -> none  [local(): lax.all_to_all(replies, 'seq', split_axis=0, concat_axis=0, tiled=True)]
  transfers between devices with their start and end apart: 4 -> 0, of which waited for: 4 -> 0; matrix products, arithmetic and copies ran while one was open for 2% -> 0% of each run, Pallas kernels for 0% -> 0%
where the time goes in v3:
time: 172 us
  Pallas kernels  166 us (97%)
  local copies, waits for them, and re-layouts  5.92 us (3%)
    pallas_call x1, Pallas kernels, layer(): pl.pallas_call(functools.partial(layer_kernel, sizes, PLAN), out_shape=ja...  166 us
    unnamed x2, local copies, waits for them, and re-layouts  3.88 us

profile of v3, /device:TPU:1, one launch (start us, length us, event | category | flops | bytes accessed | tf_op | source)
XLA Modules:
  0.0 171.6 jit_solution(5855417213588797128)
XLA Ops:
  0.0 1.3 copy.9.sorted_ref
  1.3 0.8 copy.8
  2.1 0.1 reshape_squeeze.3
  2.2 0.6 broadcast_in_dim.6.list_ref
  2.8 165.7 %layer.1 = bf16[256,4096]{1,0:T(8,128)(2,1)} custom-call(s32[8,2]{1,0:T(8,128)} %copy.9.sorted_ref, s32[8,128]{1,0:T(8,128)} %broadcast_in_dim.6.list_ref, bf16[256,4096]{1,0:T(8,128)(2,1)} %bitcast.5, bf16[256,4096]{1,0:T(8,128)(2,1)} %bitcast.6, bf16[16,1024]{1,0:T(8,128)(2,1)} %key_ref.1, bf16[16,1024]{1,0:T(8,128)(2,1)} %value_ref.1), custom_call_target="tpu_custom_call" | custom-call | tf_op jit(solution)/shard_map/layer/pallas_call | solution.py:451
  168.5 3.1 %copy.11 = bf16[1,256,4096]{2,1,0:T(8,128)(2,1)} copy(bf16[1,256,4096]{2,1,0:T(8,128)(2,1)} %bitcast.4) | data formatting | bytes 4194304
  (1 shorter events, 0.0 us)

commit v4 on v3

--- a/solution.py
+++ b/solution.py
@@ -141,13 +141,13 @@
                 yield time, more
 
 
-def gather_weight(place, copies, group, weights, kind, part, order, ready, begin, spans):
-    first, second, third = order
+def gather_weight(place, copies, group, weights, kind, part, axes, begin, spans):
+    second, third = axes
+    width = weights.shape[-1] // 2
 
     def piece(where, half):
         rows = FULL if half is None else pl.ds(half * 16, 16)
-        at = [where[axis] for axis in AXES]
-        return weights.at[kind, part, at[0], at[1], at[2], rows, :]
+        return weights.at[kind, where["x"], :, where["y"], rows, pl.ds(part * width, width)]
 
     def nothing(here, time):
         return []
@@ -156,13 +156,9 @@
         return group.add(ring(place, copies, piece, third, {**where, third: place.at[third]}, time, spans[2], nothing))
 
     def whole():
-        yield begin[0], []
-        ready(kind, part)
-        yield from ring(place, copies, piece, first, dict(place.at), begin[0], spans[0], nothing)
-        slab = {**place.at, first: FULL}
-        yield begin[1], [
-            group.add(ring(place, copies, piece, second, slab, begin[1], spans[1], lambda here, time: [third_ring(here, time)])),
-            third_ring(slab, begin[1]),
+        yield begin, [
+            group.add(ring(place, copies, piece, second, dict(place.at), begin, spans[1], lambda here, time: [third_ring(here, time)])),
+            third_ring(dict(place.at), begin),
         ]
 
     return group.add(whole())
@@ -184,8 +180,8 @@
         return [pltpu.VMEM(shape + block, jnp.bfloat16) for shape in shapes]
 
 
-def layer_kernel(sizes, plan, sorted_ref, list_ref, tokens_ref, queries_ref, key_ref, value_ref, out_ref,
-                 weights, tokens, queries, lists, wanted_vector, wanted, softmax, *rest):
+def layer_kernel(sizes, plan, list_ref, tokens_ref, queries_ref, key_ref, value_ref, out_ref,
+                 weights, tokens, queries, lists, wanted_vector, wanted, own_list, softmax, *rest):
     kinds = [Kind(rest[:13]), Kind(rest[13:26])]
     load_sem, send_sem, recv_sem = rest[26:]
     place = Place(sizes)
@@ -201,12 +197,16 @@
         loads[name] = pltpu.make_async_copy(source, target, load_sem.at[len(loads)])
         loads[name].start()
 
-    def weight_columns(ref, which, part):
-        return ref.at[:, pl.ds(pl.multiple_of(which * half_width + part * part_width, part_width), part_width)]
-
-    for kind, ref in enumerate((key_ref, value_ref)):
-        for part in range(2):
-            load((kind, part), weight_columns(ref, core, part), weights.at[kind, part, x, z, y, pl.ds(core * 16, 16), :])
+    def weight_columns(ref, which):
+        return ref.at[:, pl.ds(pl.multiple_of(which * half_width, half_width), half_width)]
+
+    def weight_rows(kind, which):
+        return weights.at[kind, x, z, y, pl.ds(which * 16, 16), :]
+
+    weight_refs = (key_ref, value_ref)
+    for kind in range(2):
+        load(kind, weight_columns(weight_refs[kind], core), weight_rows(kind, core))
+    load("own_list", list_ref, own_list)
     load("lists", list_ref, lists.at[z, y, core])
     load("tokens", tokens_ref, tokens.at[core])
     load("queries", queries_ref, queries)
@@ -220,16 +220,23 @@
     pl.semaphore_wait(barrier, len(peers))
 
     shared = {}
-    for kind, ref in enumerate((key_ref, value_ref)):
-        for part in range(2):
-            shared[kind, part] = copies.start(
-                weight_columns(ref, 1 - core, part), weights.at[kind, part, x, z, y, pl.ds(core * 16, 16), :], place.sibling()
-            )
+    for kind in range(2):
+        shared[kind] = copies.start(
+            weight_columns(weight_refs[kind], 1 - core), weight_rows(kind, core), place.sibling()
+        )
     shared["tokens"] = copies.start(tokens_ref, tokens.at[core], place.sibling())
 
-    def ready(kind, part):
-        loads[kind, part].wait()
-        copies.arrived(shared[kind, part], weights.at[kind, part, x, z, y, pl.ds((1 - core) * 16, 16), :])
+    def first_task(then):
+        for kind in range(2):
+            loads[kind].wait()
+            copies.arrived(shared[kind], weight_rows(kind, 1 - core))
+
+        def piece(where, half):
+            rows = FULL if half is None else pl.ds(half * 16, 16)
+            return weights.at[:, where["x"], where["z"], where["y"], rows, :]
+
+        yield from ring(place, copies, piece, "z", dict(place.at), *plan["first"], lambda here, time: [])
+        yield plan["first"][0] + 4 * plan["first"][1], then
 
     def list_task():
         def piece(where, half):
@@ -239,22 +246,22 @@
             return []
 
         loads["lists"].wait()
-        yield from ring(place, copies, piece, "z", dict(place.at), 0.0, 2.0, nothing, halves=False)
-        yield from ring(place, copies, piece, "y", {**place.at, "z": FULL}, 8.0, 2.0, nothing, halves=False)
+        yield from ring(place, copies, piece, "z", dict(place.at), *plan["lists"][0], nothing, halves=False)
+        yield from ring(place, copies, piece, "y", {**place.at, "z": FULL}, *plan["lists"][1], nothing, halves=False)
         mine = lists.at[:, :, core]
         ticket = copies.start(mine, mine, place.sibling())
-        yield 14.5, []
+        yield plan["lists"][2], []
         copies.arrived(ticket, lists.at[:, :, 1 - core])
         lane = lax.broadcasted_iota(jnp.int32, (8, LANES), 1)
         source = lax.broadcasted_iota(jnp.int32, (8, LANES), 0) * columns + place.column
 
         def one_device(device, total):
             tile = lists[lax.div(device, columns), lax.div(lax.rem(device, columns), 2), lax.rem(device, 2)]
-            item = (tile & 1) * KVH + (lane >> 1) + 1
+            item = (tile & 1) * KVH + (lane & 7) + 1
             found = jnp.sum(jnp.where((tile >> 1) == source, item, 0), axis=1, keepdims=True)
             return jnp.where(lane == device, found, total)
 
-        wanted_vector[...] = lax.fori_loop(0, rows_z * columns, one_device, jnp.zeros((8, LANES), jnp.int32))
+        wanted_vector[...] = lax.fori_loop(0, rows_z * columns, one_device, jnp.zeros((8, LANES), jnp.int32), unroll=8)
         copy = pltpu.make_async_copy(wanted_vector, wanted, load_sem.at[len(loads)])
         copy.start()
         copy.wait()
@@ -270,7 +277,7 @@
             loads["tokens"].wait()
             copies.arrived(shared["tokens"], tokens.at[1 - core])
         for part in range(2):
-            weight = weights[kind, part].reshape(tokens.shape[2], part_width)
+            weight = weights[kind, :, :, :, :, part * part_width : (part + 1) * part_width].reshape(tokens.shape[2], part_width)
             for mine in (False, True):
                 which = core if mine else 1 - core
                 result = jnp.dot(tokens[which], weight, preferred_element_type=jnp.float32).astype(jnp.bfloat16)
@@ -364,7 +371,7 @@
 
     def candidates(kind, block, head):
         buffers = kinds[kind]
-        device = lax.div(sorted_ref[head, block], 2)
+        device = lax.div(own_list[0, block * KVH + head], 2)
         distance = lax.rem(lax.div(device, columns) - z + rows_z, rows_z)
         slot = jnp.where(
             distance < 4, 2 * distance, jnp.where(distance == 4, 7, 2 * (rows_z - distance) - 1)
@@ -394,6 +401,7 @@
         yield wake, []
         if block == 0 and head_range[0] == 0:
             loads["queries"].wait()
+            loads["own_list"].wait()
         lax.fori_loop(*head_range, one_head, 0)
 
     def output_task():
@@ -422,27 +430,28 @@
         Group(lambda wake: exchange(0, softmax_tasks)),
         Group(lambda wake: exchange(1, [values_ready])),
     ]
-    tasks = [list_task()]
-    for kind in range(2):
-        for part, order in enumerate((("z", "y", "x"), ("z", "x", "y"))):
-            tasks.append(
-                gather_weight(place, copies, groups[kind], weights, kind, part, order, ready, plan["begin"][kind], plan["spans"])
-            )
+    gathers = [
+        gather_weight(place, copies, groups[kind], weights, kind, part, axes, plan["begin"][kind], plan["spans"])
+        for kind in range(2) for part, axes in enumerate((("y", "x"), ("x", "y")))
+    ]
+    tasks = [first_task(gathers), list_task()]
     run_tasks(tasks)
     copies.sent()
     assert len(copies.started) == COPIES, len(copies.started)
 
 
 PLAN = {
-    "begin": ((0.0, 10.0), (0.5, 27.0)),
-    "spans": (2.0, 5.0, 8.0),
-    "exchange": ((36.0, 48.0, 60.0, 69.0, 73.0, 78.0), (64.0, 82.0, 94.0, 104.0, 108.0, 114.0)),
-    "softmax": (78.5, 82.5, 86.0, 95.0),
-    "output": 115.0,
+    "first": (0.1, 2.4),
+    "lists": ((0.2, 2.4), (14.2, 4.0), 44.5),
+    "begin": (10.0, 44.0),
+    "spans": (2.0, 5.0, 9.0),
+    "exchange": ((43.0, 53.0, 66.0, 79.0, 83.0, 88.0), (74.0, 84.0, 96.0, 107.0, 111.0, 116.0)),
+    "softmax": (88.5, 90.5, 97.0, 99.0),
+    "output": 117.0,
 }
 
 
-def layer(sorted_blocks, lists, tokens, queries, key_weight, value_weight, sizes):
+def layer(lists, tokens, queries, key_weight, value_weight, sizes):
     local_tokens, depth = tokens.shape
     part_rows, width = key_weight.shape
     columns, rows = 2 * sizes["y"], sizes["z"]
@@ -451,14 +460,15 @@
     return pl.pallas_call(
         functools.partial(layer_kernel, sizes, PLAN),
         out_shape=jax.ShapeDtypeStruct(queries.shape, jnp.bfloat16),
-        in_specs=[pl.BlockSpec(memory_space=pltpu.SMEM)] + [hbm] * 5,
+        in_specs=[hbm] * 5,
         out_specs=pl.BlockSpec(memory_space=pltpu.VMEM),
         scratch_shapes=[
-            pltpu.VMEM((2, 2, sizes["x"], rows, sizes["y"], 2 * part_rows, width // 4), jnp.bfloat16),
+            pltpu.VMEM((2, sizes["x"], rows, sizes["y"], 2 * part_rows, width // 2), jnp.bfloat16),
             pltpu.VMEM((2, local_tokens, depth), jnp.bfloat16),
             pltpu.VMEM(queries.shape, jnp.bfloat16),
             pltpu.VMEM((rows, sizes["y"], 2, 8, LANES), jnp.int32),
             pltpu.VMEM((8, LANES), jnp.int32),
+            pltpu.SMEM((8, LANES), jnp.int32),
             pltpu.SMEM((8, LANES), jnp.int32),
             pltpu.VMEM((2 * KVH, GROUP * BLOCK, 3 * BLOCK), jnp.bfloat16),
             *kind,
@@ -471,18 +481,18 @@
             collective_id=0, has_side_effects=True, vmem_limit_bytes=58 << 20
         ),
         name="layer",
-    )(sorted_blocks, lists, tokens, queries, key_weight, value_weight)
-
-
-COPIES = 204
+    )(lists, tokens, queries, key_weight, value_weight)
+
+
+COPIES = 178
 
 
 def local(tokens, queries, key_weight, value_weight, sorted_blocks):
     devices = lax.axis_size("seq")
     sizes = {"x": lax.axis_size("fsdp"), "y": 4, "z": devices // 8}
-    own = sorted_blocks[0].reshape(-1)
+    own = sorted_blocks[0].T.reshape(-1)
     lists = jnp.broadcast_to(jnp.pad(own, (0, LANES - own.shape[0]), constant_values=-1), (8, LANES))
-    return layer(sorted_blocks[0], lists, tokens[0], queries[0], key_weight, value_weight, sizes)[None]
+    return layer(lists, tokens[0], queries[0], key_weight, value_weight, sizes)[None]
 
 
 def solution(mesh):

time: 172 us -> 160 us (0.930)
  Pallas kernels: 166 us -> 155 us
    pallas_call x1, Pallas kernels: 166 us -> 155 us  [layer(): pl.pallas_call(functools.partial(layer_kernel, sizes, PLAN), out_shape=ja...]
    unnamed x2 -> x1, local copies, waits for them, and re-layouts: 3.88 us -> 3.13 us
where the time goes in v4:
time: 160 us; the launch traced here: 159 us
  Pallas kernels  155 us (97%)
  local copies, waits for them, and re-layouts  4.49 us (3%)
    pallas_call x1, Pallas kernels, layer(): pl.pallas_call(functools.partial(layer_kernel, sizes, PLAN), out_shape=ja...  155 us

profile of v4, /device:TPU:1, one launch (start us, length us, event | category | flops | bytes accessed | tf_op | source)
XLA Modules:
  0.0 159.4 jit_solution(13511030863934778870)
XLA Ops:
  0.0 0.8 reshape.3
  0.8 0.6 broadcast_in_dim.6.list_ref
  1.4 154.9 %layer.1 = bf16[256,4096]{1,0:T(8,128)(2,1)} custom-call(s32[8,128]{1,0:T(8,128)} %broadcast_in_dim.6.list_ref, bf16[256,4096]{1,0:T(8,128)(2,1)} %bitcast.7, bf16[256,4096]{1,0:T(8,128)(2,1)} %bitcast.8, bf16[16,1024]{1,0:T(8,128)(2,1)} %key_ref.1, bf16[16,1024]{1,0:T(8,128)(2,1)} %value_ref.1), custom_call_target="tpu_custom_call" | custom-call | tf_op jit(solution)/shard_map/layer/pallas_call | solution.py:460
  156.3 3.1 %copy.7 = bf16[1,256,4096]{2,1,0:T(8,128)(2,1)} copy(bf16[1,256,4096]{2,1,0:T(8,128)(2,1)} %bitcast.6) | data formatting | bytes 4194304
  (1 shorter events, 0.0 us)

commit v5 on v4

--- a/solution.py
+++ b/solution.py
@@ -16,7 +16,7 @@
 AXES = ("x", "z", "y")
 FULL = slice(None)
 LANES = 128
-STAGES = ((0, 3), (3, 5), (5, 7), (7, 8))
+STAGES = (((0, 0), (0, 5), (5, 7), (7, 8)), ((0, 3), (3, 5), (5, 7), (7, 8)))
 
 
 class Place:
@@ -181,7 +181,7 @@
 
 
 def layer_kernel(sizes, plan, list_ref, tokens_ref, queries_ref, key_ref, value_ref, out_ref,
-                 weights, tokens, queries, lists, wanted_vector, wanted, own_list, softmax, *rest):
+                 weights, tokens, queries, lists, wanted_vector, wanted, own_list, softmax, partial, *rest):
     kinds = [Kind(rest[:13]), Kind(rest[13:26])]
     load_sem, send_sem, recv_sem = rest[26:]
     place = Place(sizes)
@@ -224,7 +224,6 @@
         shared[kind] = copies.start(
             weight_columns(weight_refs[kind], 1 - core), weight_rows(kind, core), place.sibling()
         )
-    shared["tokens"] = copies.start(tokens_ref, tokens.at[core], place.sibling())
 
     def first_task(then):
         for kind in range(2):
@@ -236,6 +235,7 @@
             return weights.at[:, where["x"], where["z"], where["y"], rows, :]
 
         yield from ring(place, copies, piece, "z", dict(place.at), *plan["first"], lambda here, time: [])
+        shared["tokens"] = copies.start(tokens_ref, tokens.at[core], place.sibling())
         yield plan["first"][0] + 4 * plan["first"][1], then
 
     def list_task():
@@ -290,8 +290,11 @@
                             buffers.swap[block, part * 2 + head] = value
         return copies.start(buffers.swap, buffers.own.at[:, pl.ds(core * (KVH // 2), KVH // 2)], place.sibling())
 
-    def send_slots(buffers, stage, row_tickets):
-        begin, end = STAGES[stage]
+    def send_slots(kind, stage, row_tickets):
+        buffers = kinds[kind]
+        begin, end = STAGES[kind][stage]
+        if begin == end:
+            return
         sources = {0: (buffers.own, 0), 1: (buffers.back1, -1), 2: (buffers.ahead1, 1), 3: (buffers.back2, -2), 4: (buffers.ahead2, 2)}
 
         def value(slot, column):
@@ -343,43 +346,48 @@
             ahead = copies.start(buffers.back1, buffers.back2, place.device("z", 1))
             copies.arrived(behind, buffers.ahead1)
             behind = copies.start(buffers.ahead1, buffers.ahead2, place.device("z", -1))
-            send_slots(buffers, 0, row_tickets)
+            send_slots(kind, 0, row_tickets)
             yield times[2], []
             copies.arrived(ahead, buffers.back2)
             ahead = send_far(buffers, 1)
             copies.arrived(behind, buffers.ahead2)
             behind = send_far(buffers, -1)
-            send_slots(buffers, 1, row_tickets)
+            send_slots(kind, 1, row_tickets)
             yield times[3], []
             tail = pl.ds(columns, columns // 2)
             copies.arrived(ahead, buffers.far_back)
             ahead = copies.start(buffers.far_back.at[tail], buffers.last.at[0], place.device("z", 1))
             copies.arrived(behind, buffers.far_ahead)
             behind = copies.start(buffers.far_ahead.at[tail], buffers.last.at[1], place.device("z", -1))
-            send_slots(buffers, 2, row_tickets)
+            send_slots(kind, 2, row_tickets)
             yield times[4], []
             copies.arrived(ahead, buffers.last.at[0])
             copies.arrived(behind, buffers.last.at[1])
-            send_slots(buffers, 3, row_tickets)
+            send_slots(kind, 3, row_tickets)
+            if kind == 1:
+                copies.arrived(edge, buffers.edge)
+                partial_output()
             yield times[5], []
-            copies.arrived(edge, buffers.edge)
+            if kind == 0:
+                copies.arrived(edge, buffers.edge)
             for ticket, target in row_tickets:
                 copies.arrived(ticket, target)
             yield times[5], then
 
         return [task()]
 
-    def candidates(kind, block, head):
+    def near_pair(kind, block, head):
         buffers = kinds[kind]
+        before = buffers.edge[head] if block == 0 else buffers.own[0, head]
+        return [buffers.own[block, head], before]
+
+    def chosen(kind, block, head):
         device = lax.div(own_list[0, block * KVH + head], 2)
         distance = lax.rem(lax.div(device, columns) - z + rows_z, rows_z)
         slot = jnp.where(
             distance < 4, 2 * distance, jnp.where(distance == 4, 7, 2 * (rows_z - distance) - 1)
         )
-        before = buffers.edge[head] if block == 0 else buffers.own[0, head]
-        return jnp.concatenate(
-            [buffers.own[block, head], before, buffers.arrived[lax.rem(device, columns), slot]], axis=0
-        )
+        return kinds[kind].arrived[lax.rem(device, columns), slot]
 
     def weights_task(block, head_range, wake):
         def one_head(head, carry):
@@ -387,7 +395,7 @@
             query = queries[rows, pl.ds(pl.multiple_of(head * GROUP * DH, GROUP * DH), GROUP * DH)]
             query = jnp.concatenate([query[:, g * DH : (g + 1) * DH] for g in range(GROUP)], axis=0)
             scores = lax.dot_general(
-                query, candidates(0, block, head), (((1,), (1,)), ((), ())), preferred_element_type=jnp.float32
+                query, jnp.concatenate(near_pair(0, block, head) + [chosen(0, block, head)], axis=0), (((1,), (1,)), ((), ())), preferred_element_type=jnp.float32
             ) * (math.log2(math.e) / math.sqrt(DH))
             if block == 0:
                 index = lax.broadcasted_iota(jnp.int32, scores.shape, 1)
@@ -404,14 +412,29 @@
             loads["own_list"].wait()
         lax.fori_loop(*head_range, one_head, 0)
 
+    def partial_output():
+        for block in range(2):
+
+            def one_head(head, carry, block=block):
+                item = block * KVH + head
+                partial[item] = jnp.dot(
+                    softmax[item, :, : 2 * BLOCK], jnp.concatenate(near_pair(1, block, head), axis=0),
+                    preferred_element_type=jnp.float32,
+                )
+                return carry
+
+            lax.fori_loop(0, KVH, one_head, 0)
+
     def output_task():
         yield plan["output"], []
         for block in range(2):
 
             def one_head(head, carry, block=block):
-                result = jnp.dot(
-                    softmax[block * KVH + head], candidates(1, block, head), preferred_element_type=jnp.float32
-                ).astype(jnp.bfloat16)
+                item = block * KVH + head
+                result = partial[item] + jnp.dot(
+                    softmax[item, :, 2 * BLOCK :], chosen(1, block, head), preferred_element_type=jnp.float32
+                )
+                result = result.astype(jnp.bfloat16)
                 for g in range(GROUP):
                     lanes = pl.ds(pl.multiple_of((head * GROUP + g) * DH, DH), DH)
                     out_ref[block * BLOCK : (block + 1) * BLOCK, lanes] = result[g * BLOCK : (g + 1) * BLOCK]
@@ -471,6 +494,7 @@
             pltpu.SMEM((8, LANES), jnp.int32),
             pltpu.SMEM((8, LANES), jnp.int32),
             pltpu.VMEM((2 * KVH, GROUP * BLOCK, 3 * BLOCK), jnp.bfloat16),
+            pltpu.VMEM((2 * KVH, GROUP * BLOCK, DH), jnp.float32),
             *kind,
             *kind,
             pltpu.SemaphoreType.DMA((8,)),
@@ -484,7 +508,7 @@
     )(lists, tokens, queries, key_weight, value_weight)
 
 
-COPIES = 178
+COPIES = 171
 
 
 def local(tokens, queries, key_weight, value_weight, sorted_blocks):

time: 160 us -> 151 us (0.944)
  Pallas kernels: 155 us -> 146 us
    pallas_call x1, Pallas kernels: 155 us -> 146 us  [layer(): pl.pallas_call(functools.partial(layer_kernel, sizes, PLAN), out_shape=ja...]
where the time goes in v5:
time: 151 us
  Pallas kernels  146 us (97%)
  local copies, waits for them, and re-layouts  4.49 us (3%)
    pallas_call x1, Pallas kernels, layer(): pl.pallas_call(functools.partial(layer_kernel, sizes, PLAN), out_shape=ja...  146 us
    unnamed x1, local copies, waits for them, and re-layouts  3.13 us

profile of v5, /device:TPU:1, one launch (start us, length us, event | category | flops | bytes accessed | tf_op | source)
XLA Modules:
  0.0 150.7 jit_solution(6505773242403320843)
XLA Ops:
  0.0 0.8 reshape.3
  0.8 0.6 broadcast_in_dim.6.list_ref
  1.4 146.2 %layer.1 = bf16[256,4096]{1,0:T(8,128)(2,1)} custom-call(s32[8,128]{1,0:T(8,128)} %broadcast_in_dim.6.list_ref, bf16[256,4096]{1,0:T(8,128)(2,1)} %bitcast.7, bf16[256,4096]{1,0:T(8,128)(2,1)} %bitcast.8, bf16[16,1024]{1,0:T(8,128)(2,1)} %key_ref.1, bf16[16,1024]{1,0:T(8,128)(2,1)} %value_ref.1), custom_call_target="tpu_custom_call" | custom-call | tf_op jit(solution)/shard_map/layer/pallas_call | solution.py:483
  147.6 3.1 %copy.7 = bf16[1,256,4096]{2,1,0:T(8,128)(2,1)} copy(bf16[1,256,4096]{2,1,0:T(8,128)(2,1)} %bitcast.6) | data formatting | bytes 4194304
  (1 shorter events, 0.0 us)

commit v6 on v5

--- a/solution.py
+++ b/solution.py
@@ -16,7 +16,8 @@
 AXES = ("x", "z", "y")
 FULL = slice(None)
 LANES = 128
-STAGES = (((0, 0), (0, 5), (5, 7), (7, 8)), ((0, 3), (3, 5), (5, 7), (7, 8)))
+HALF_HOP = 5.0
+STAGES = (((0, 0), (0, 0), (0, 7), (7, 8)), ((0, 3), (3, 5), (5, 7), (7, 8)))
 
 
 class Place:
@@ -225,18 +226,20 @@
             weight_columns(weight_refs[kind], 1 - core), weight_rows(kind, core), place.sibling()
         )
 
-    def first_task(then):
-        for kind in range(2):
-            loads[kind].wait()
-            copies.arrived(shared[kind], weight_rows(kind, 1 - core))
+    def first_task(kind, then):
+        begin, span = plan["first"][kind]
+        yield begin, []
+        loads[kind].wait()
+        copies.arrived(shared[kind], weight_rows(kind, 1 - core))
 
         def piece(where, half):
             rows = FULL if half is None else pl.ds(half * 16, 16)
-            return weights.at[:, where["x"], where["z"], where["y"], rows, :]
-
-        yield from ring(place, copies, piece, "z", dict(place.at), *plan["first"], lambda here, time: [])
-        shared["tokens"] = copies.start(tokens_ref, tokens.at[core], place.sibling())
-        yield plan["first"][0] + 4 * plan["first"][1], then
+            return weights.at[kind, where["x"], where["z"], where["y"], rows, :]
+
+        yield from ring(place, copies, piece, "z", dict(place.at), begin, span, lambda here, time: [])
+        if kind == 0:
+            shared["tokens"] = copies.start(tokens_ref, tokens.at[core], place.sibling())
+        yield begin + 4 * span, then
 
     def list_task():
         def piece(where, half):
@@ -276,11 +279,13 @@
         if kind == 0:
             loads["tokens"].wait()
             copies.arrived(shared["tokens"], tokens.at[1 - core])
-        for part in range(2):
-            weight = weights[kind, :, :, :, :, part * part_width : (part + 1) * part_width].reshape(tokens.shape[2], part_width)
-            for mine in (False, True):
-                which = core if mine else 1 - core
-                result = jnp.dot(tokens[which], weight, preferred_element_type=jnp.float32).astype(jnp.bfloat16)
+        for mine in (False, True):
+            for part in range(2):
+                weight = weights[kind, :, :, :, :, part * part_width : (part + 1) * part_width]
+                result = jnp.dot(
+                    tokens[core if mine else 1 - core], weight.reshape(tokens.shape[2], part_width),
+                    preferred_element_type=jnp.float32,
+                ).astype(jnp.bfloat16)
                 for block in range(2):
                     for head in range(2):
                         value = result[block * BLOCK : (block + 1) * BLOCK, head * DH : (head + 1) * DH]
@@ -288,7 +293,11 @@
                             buffers.own[block, core * (KVH // 2) + part * 2 + head] = value
                         else:
                             buffers.swap[block, part * 2 + head] = value
-        return copies.start(buffers.swap, buffers.own.at[:, pl.ds(core * (KVH // 2), KVH // 2)], place.sibling())
+            if not mine:
+                ticket = copies.start(
+                    buffers.swap, buffers.own.at[:, pl.ds(core * (KVH // 2), KVH // 2)], place.sibling()
+                )
+        return ticket
 
     def send_slots(kind, stage, row_tickets):
         buffers = kinds[kind]
@@ -336,21 +345,31 @@
             buffers = kinds[kind]
             row_tickets = []
             ticket = project(kind)
-            yield times[0], []
-            copies.arrived(ticket, buffers.own.at[:, pl.ds((1 - core) * (KVH // 2), KVH // 2)])
-            ahead = copies.start(buffers.own, buffers.back1, place.device("z", 1))
-            behind = copies.start(buffers.own, buffers.ahead1, place.device("z", -1))
+            sides = [pl.ds(core * (KVH // 2), KVH // 2), pl.ds((1 - core) * (KVH // 2), KVH // 2)]
+            hops = ((buffers.own, buffers.back1, buffers.back2, 1), (buffers.own, buffers.ahead1, buffers.ahead2, -1))
+            first_hop, second_hop = [], []
+            for side in range(2):
+                if side == 1:
+                    yield times[0], []
+                    copies.arrived(ticket, buffers.own.at[:, sides[1]])
+                for source, near, _, direction in hops:
+                    ticket_near = copies.start(source.at[:, sides[side]], near.at[:, sides[side]], place.device("z", direction))
+                    first_hop.append(ticket_near)
             edge = copies.start(buffers.own.at[1], buffers.edge, place.along(1))
-            yield times[1], []
-            copies.arrived(ahead, buffers.back1)
-            ahead = copies.start(buffers.back1, buffers.back2, place.device("z", 1))
-            copies.arrived(behind, buffers.ahead1)
-            behind = copies.start(buffers.ahead1, buffers.ahead2, place.device("z", -1))
+            for side in range(2):
+                yield times[1] - (HALF_HOP if side == 0 else 0.0), []
+                for index, (_, near, far, direction) in enumerate(hops):
+                    copies.arrived(first_hop[side * 2 + index], near.at[:, sides[side]])
+                    second_hop.append(
+                        copies.start(near.at[:, sides[side]], far.at[:, sides[side]], place.device("z", direction))
+                    )
             send_slots(kind, 0, row_tickets)
             yield times[2], []
-            copies.arrived(ahead, buffers.back2)
+            for side in range(2):
+                copies.arrived(second_hop[side * 2], buffers.back2.at[:, sides[side]])
             ahead = send_far(buffers, 1)
-            copies.arrived(behind, buffers.ahead2)
+            for side in range(2):
+                copies.arrived(second_hop[side * 2 + 1], buffers.ahead2.at[:, sides[side]])
             behind = send_far(buffers, -1)
             send_slots(kind, 1, row_tickets)
             yield times[3], []
@@ -454,22 +473,25 @@
         Group(lambda wake: exchange(1, [values_ready])),
     ]
     gathers = [
-        gather_weight(place, copies, groups[kind], weights, kind, part, axes, plan["begin"][kind], plan["spans"])
-        for kind in range(2) for part, axes in enumerate((("y", "x"), ("x", "y")))
+        [
+            gather_weight(place, copies, groups[kind], weights, kind, part, axes, plan["begin"][kind], plan["spans"])
+            for part, axes in enumerate((("y", "x"), ("x", "y")))
+        ]
+        for kind in range(2)
     ]
-    tasks = [first_task(gathers), list_task()]
+    tasks = [first_task(0, gathers[0]), list_task(), first_task(1, gathers[1])]
     run_tasks(tasks)
     copies.sent()
     assert len(copies.started) == COPIES, len(copies.started)
 
 
 PLAN = {
-    "first": (0.1, 2.4),
+    "first": ((0.1, 2.4), (10.5, 3.0)),
     "lists": ((0.2, 2.4), (14.2, 4.0), 44.5),
     "begin": (10.0, 44.0),
     "spans": (2.0, 5.0, 9.0),
-    "exchange": ((43.0, 53.0, 66.0, 79.0, 83.0, 88.0), (74.0, 84.0, 96.0, 107.0, 111.0, 116.0)),
-    "softmax": (88.5, 90.5, 97.0, 99.0),
+    "exchange": ((43.0, 53.0, 66.0, 79.0, 83.0, 96.5), (74.0, 84.0, 96.0, 107.0, 111.0, 116.0)),
+    "softmax": (97.0, 98.0, 99.0, 100.0),
     "output": 117.0,
 }
 
@@ -508,7 +530,7 @@
     )(lists, tokens, queries, key_weight, value_weight)
 
 
-COPIES = 171
+COPIES = 180
 
 
 def local(tokens, queries, key_weight, value_weight, sorted_blocks):

time: 151 us -> 147 us (0.974)
  Pallas kernels: 146 us -> 142 us
    pallas_call x1, Pallas kernels: 146 us -> 142 us  [layer(): pl.pallas_call(functools.partial(layer_kernel, sizes, PLAN), out_shape=ja...]
where the time goes in v6:
time: 147 us
  Pallas kernels  142 us (97%)
  local copies, waits for them, and re-layouts  4.49 us (3%)
    pallas_call x1, Pallas kernels, layer(): pl.pallas_call(functools.partial(layer_kernel, sizes, PLAN), out_shape=ja...  142 us
    unnamed x1, local copies, waits for them, and re-layouts  3.13 us

profile of v6, /device:TPU:1, one launch (start us, length us, event | category | flops | bytes accessed | tf_op | source)
XLA Modules:
  0.0 146.7 jit_solution(16591603489239986234)
XLA Ops:
  0.0 0.8 reshape.3
  0.8 0.6 broadcast_in_dim.6.list_ref
  1.4 142.2 %layer.1 = bf16[256,4096]{1,0:T(8,128)(2,1)} custom-call(s32[8,128]{1,0:T(8,128)} %broadcast_in_dim.6.list_ref, bf16[256,4096]{1,0:T(8,128)(2,1)} %bitcast.7, bf16[256,4096]{1,0:T(8,128)(2,1)} %bitcast.8, bf16[16,1024]{1,0:T(8,128)(2,1)} %key_ref.1, bf16[16,1024]{1,0:T(8,128)(2,1)} %value_ref.1), custom_call_target="tpu_custom_call" | custom-call | tf_op jit(solution)/shard_map/layer/pallas_call | solution.py:505
  143.6 3.1 %copy.7 = bf16[1,256,4096]{2,1,0:T(8,128)(2,1)} copy(bf16[1,256,4096]{2,1,0:T(8,128)(2,1)} %bitcast.6) | data formatting | bytes 4194304
  (1 shorter events, 0.0 us)
